TPU v7x, 512 devices: a whole 4x8x8 slice. The times are simulated.
512 devices in a mesh: stream: 16 (over y, core), cell: 32 (over x, z).
Axes of the slice: x: 4, y: 8, z: 8, core: 2. Of those that a mesh axis runs over, the one named last changes fastest.
Arguments:
- positions: float32 [16, 1024, 3, 128], P('stream', 'cell'), may hold values from 0 to 2
- strengths: float32 [16, 1024, 3, 128], P('stream', 'cell'), may hold values from -4 to 4
- fill: int32 [16, 1024], P('stream', 'cell'), may hold values from 64 to 128
- export_cells: int32 [16, 32, 32, 2], P('stream', 'cell'), may hold values from 0 to 31
- pair_local: int32 [16, 6144], P('stream', 'cell'), may hold values from 0 to 31
- pair_remote: int32 [16, 6144], P('stream', 'cell'), may hold values from 0 to 63
- pair_count: int32 [16, 32], P('stream', 'cell'), may hold values from 64 to 192
Outputs:
- new_positions: float32 [16, 1024, 3, 128], P('stream', 'cell')
- new_strengths: float32 [16, 1024, 3, 128], P('stream', 'cell')
All inputs are finite; a program needn't handle non-finite values.
Results may differ from a plain program's by a relative error of at most 0.00016.
Values sent between devices are 32-bit elements; how exact they have to be, the bound alone decides.
No kernel may reach another device: no remote copies, remote signals or barrier semaphores. Data moves between devices by JAX's collectives and lax.ppermute only.
A program may use at most 64 MiB of HBM per device.

v0:
```python
import math

import jax
import jax.numpy as jnp
from jax import lax
from jax.sharding import PartitionSpec as P

sigma_sq = 0.09
spread_inv = 3.125
viscous = 0.01
time_step = 0.2
kernel_scale = 1.0 / (4.0 * math.pi)


def shifted(value, axis, steps):
    count = lax.axis_size(axis)
    leading, last = (max(0, -steps), min(count, count - steps))
    return lax.ppermute(value, axis, [(source, source + steps) for source in range(leading, last)])


def cross_product(left, right):
    return [
        left[1] * right[2] - left[2] * right[1],
        left[2] * right[0] - left[0] * right[2],
        left[0] * right[1] - left[1] * right[0],
    ]


def pair_terms(first, second, both):
    here_pos = [first[:, k, :, None] for k in range(3)]
    there_pos = [second[:, k, None, :] for k in range(3)]
    here_str = [first[:, 3 + k, :, None] for k in range(3)]
    there_str = [second[:, 3 + k, None, :] for k in range(3)]
    here_mask = first[:, 6, :, None]
    there_mask = second[:, 6, None, :]
    sep = [here_pos[k] - there_pos[k] for k in range(3)]
    dist = sep[0] * sep[0] + sep[1] * sep[1] + sep[2] * sep[2]
    soft = dist + sigma_sq
    inverse = lax.rsqrt(soft)
    cubic = inverse * inverse * inverse
    quintic = cubic / soft
    smooth = jnp.exp(-spread_inv * dist)
    cross_there = cross_product(sep, there_str)
    twist = cross_product(here_str, there_str)
    dot_here = here_str[0] * sep[0] + here_str[1] * sep[1] + here_str[2] * sep[2]
    weight_there = there_mask * smooth
    rows = [-kernel_scale * jnp.sum(cubic * cross_there[k], axis=-1) for k in range(3)]
    rows += [
        -kernel_scale
        * jnp.sum(cubic * twist[k] - 3.0 * quintic * dot_here * cross_there[k], axis=-1)
        + viscous * jnp.sum(weight_there * (there_str[k] - here_str[k]), axis=-1)
        for k in range(3)
    ]
    result_here = jnp.stack(rows, axis=1)
    if not both:
        return (result_here, None)
    cross_here = cross_product(sep, here_str)
    dot_there = there_str[0] * sep[0] + there_str[1] * sep[1] + there_str[2] * sep[2]
    weight_here = here_mask * smooth
    rows = [kernel_scale * jnp.sum(cubic * cross_here[k], axis=-2) for k in range(3)]
    rows += [
        -kernel_scale
        * jnp.sum(-cubic * twist[k] - 3.0 * quintic * dot_there * cross_here[k], axis=-2)
        + viscous * jnp.sum(weight_here * (here_str[k] - there_str[k]), axis=-2)
        for k in range(3)
    ]
    return (result_here, jnp.stack(rows, axis=1))


def local(positions, strengths, fill, export_cells, pair_local, pair_remote, pair_count):
    places = positions[0]
    vortices = strengths[0]
    cells = places.shape[0]
    width = places.shape[2]
    slots = jnp.arange(width, dtype=jnp.int32)
    mask = (slots[None, :] < fill[0][:, None]).astype(jnp.float32)
    exports = export_cells[0, 0]
    owners = exports.shape[0]
    per_owner = exports.shape[1]
    imports = owners * per_owner
    flat_exports = exports.reshape(-1)
    cell_ids = jnp.arange(cells, dtype=jnp.int32)
    import_ids = jnp.arange(imports, dtype=jnp.int32)
    local_ids = pair_local[0]
    remote_ids = pair_remote[0]
    count = pair_count[0, 0]
    lists = lax.all_gather(export_cells, "cell", axis=1, tiled=True)
    mine = lists[0][:, lax.axis_index("cell"), :]
    slab_rows = (jnp.arange(owners, dtype=jnp.int32)[:, None] * cells + mine).reshape(-1)

    def rate(here_places, here_vortices):
        packed = jnp.concatenate(
            [here_places, here_vortices * mask[:, None, :], mask[:, None, :]], axis=1
        )
        slab = lax.all_gather(packed, "cell", axis=0, tiled=True)
        imported = slab[slab_rows]
        blocks = packed.reshape(cells // 8, 8, 7, width)
        own = lax.map(lambda block: pair_terms(block, block, False)[0], blocks).reshape(
            cells, 6, width
        )
        upstream = shifted(packed, "stream", 1)
        up_blocks = upstream.reshape(cells // 8, 8, 7, width)
        near, far = lax.map(
            lambda joined: pair_terms(joined[0], joined[1], True), (blocks, up_blocks)
        )
        own = own + near.reshape(cells, 6, width)
        own = own + shifted(far.reshape(cells, 6, width), "stream", -1)

        def advance(blk, carry):
            own_acc, gained_acc = carry
            offset = blk * 8
            ids_here = lax.dynamic_slice_in_dim(local_ids, offset, 8)
            ids_there = lax.dynamic_slice_in_dim(remote_ids, offset, 8)
            alive = (offset + jnp.arange(8, dtype=jnp.int32) < count).astype(jnp.float32)
            near, far = pair_terms(packed[ids_here], imported[ids_there], True)
            pick_here = (ids_here[:, None] == cell_ids[None, :]).astype(jnp.float32) * alive[
                :, None
            ]
            pick_there = (ids_there[:, None] == import_ids[None, :]).astype(jnp.float32) * alive[
                :, None
            ]
            own_acc = own_acc + jnp.einsum(
                "nc,nkp->ckp", pick_here, near, precision=lax.Precision.HIGHEST
            )
            gained_acc = gained_acc + jnp.einsum(
                "nc,nkp->ckp", pick_there, far, precision=lax.Precision.HIGHEST
            )
            return (own_acc, gained_acc)

        rounds = (count + 7) // 8
        own, gained = lax.fori_loop(
            0, rounds, advance, (own, jnp.zeros((imports, 6, width), jnp.float32))
        )
        returned = lax.all_to_all(
            gained.reshape(owners, per_owner, 6, width),
            "cell",
            split_axis=0,
            concat_axis=0,
            tiled=True,
        )
        returned = returned.reshape(imports, 6, width)
        pick_owned = (flat_exports[:, None] == cell_ids[None, :]).astype(jnp.float32)
        own = own + jnp.einsum("ic,ikp->ckp", pick_owned, returned, precision=lax.Precision.HIGHEST)
        return own * mask[:, None, :]

    first = rate(places, vortices)
    mid_places = places + time_step * first[:, 0:3]
    mid_vortices = vortices + time_step * first[:, 3:6]
    second = rate(mid_places, mid_vortices)
    new_places = places + 0.5 * time_step * (first[:, 0:3] + second[:, 0:3])
    new_vortices = vortices + 0.5 * time_step * (first[:, 3:6] + second[:, 3:6])
    return (new_places[None], new_vortices[None])


def solution(mesh):
    in_specs = (
        P("stream", "cell", None, None),
        P("stream", "cell", None, None),
        P("stream", "cell"),
        P("stream", "cell", None, None),
        P("stream", "cell"),
        P("stream", "cell"),
        P("stream", "cell"),
    )
    out_specs = (P("stream", "cell", None, None), P("stream", "cell", None, None))
    return jax.shard_map(local, mesh=mesh, in_specs=in_specs, out_specs=out_specs, check_vma=False)
```

profile of v0, /device:TPU:8, one launch (start us, length us, event | category | flops | bytes accessed | tf_op | source)
XLA Modules:
  0.0 560.4 jit_solution(1154511963745686375)
XLA Ops:
  17.6 11.1 %while.70 = (s32[]{:T(128)}, f32[4,8,6,128]{3,1,2,0:T(8,128)S(1)}, f32[4,8,7,128]{3,1,2,0:T(8,128)S(1)}, s32[]{:T(128)}) while((s32[]{:T(128)}, f32[4,8,6,128]{3,1,2,0:T(8,128)S(1)}, f32[4,8,7,128]{3,1,2,0:T(8,128)S(1)}, s32[]{:T(128)}) %tuple.318), condition=%wide.region_10.11_spmd, body=%wide.region_0.10_spmd.sunk | while | flops 8653825 | bytes 290877 | solution.py:98
  28.7 49.0 %all_gather.10 = s32[1,32,32,2]{2,3,0,1:T(2,128)S(1)} all-gather(s32[1,1,32,2]{2,3,0,1:T(2,128)S(1)} %bitcast.598), channel_id=1, replica_groups=mesh['stream'=16,'cell'=32] {'cell'}, dimensions={1}, use_global_device_ids=true | all-gather | bytes 8448 | tf_op jit(solution)/shard_map/all_gather | solution.py:87
  78.8 15.3 %while.71 = (s32[]{:T(128)}, f32[4,8,6,128]{3,1,2,0:T(8,128)S(1)}, f32[4,8,6,128]{3,1,0,2:T(8,128)S(1)}, f32[4,8,7,128]{3,1,2,0:T(8,128)S(1)}, f32[4,8,7,128]{3,1,0,2:T(8,128)S(1)}, /*index=5*/s32[]{:T(128)}) while((s32[]{:T(128)}, f32[4,8,6,128]{3,1,2,0:T(8,128)S(1)}, f32[4,8,6,128]{3,1,0,2:T(8,128)S(1)}, f32[4,8,7,128]{3,1,2,0:T(8,128)S(1)}, ...), condition=%wide.region_30.31_spmd, body=%wide.region_11.30_spmd.sunk | while | flops 14424064 | bytes 581717 | solution.py:103
  98.3 6.1 %all-gather.3.cloned.1.call-done = f32[1024,7,128]{2,0,1:T(8,128)} async-done(((f32[32,7,128]{2,0,1:T(8,128)}), f32[1024,7,128]{2,0,1:T(8,128)}) %all-gather.3.cloned.1.call-update) | async-done | bytes 3670032 | tf_op jit(solution)/shard_map/all_gather | solution.py:95
  104.4 6.1 %copy.157 = f32[1024,7,128]{2,1,0:T(8,128)} copy(f32[1024,7,128]{2,0,1:T(8,128)} %all-gather.3.cloned.1.call-done) | data formatting | bytes 7340032 | tf_op jit(solution)/shard_map/all_gather | solution.py:95
  113.4 104.9 %while.74 = (s32[]{:T(128)}, f32[32,6,128]{2,0,1:T(8,128)S(1)}, f32[64,6,128]{2,0,1:T(8,128)S(1)}, s32[]{:T(128)}, s32[192]{0:T(256)S(1)}, /*index=5*/s32[]{:T(1...) while((s32[]{:T(128)}, f32[32,6,128]{2,0,1:T(8,128)S(1)}, ...), condition=%wide.region_50.51_spmd.clone, body=%wide.region_31.50_spmd.clone.sunk | while | flops 21579340 | bytes 1131159 | solution.py:131
  147.5 3.6 fusion.346
  219.0 57.8 %all-to-all-start = ((f32[32,2,6,128]{3,1,2,0:T(2,128)}), f32[32,2,6,128]{3,1,2,0:T(2,128)S(1)}, u32[]{:S(2)}, u32[]{:S(2)}) async-start(f32[32,2,6,128]{3,1,2,0:T(2,128)} %copy.160), calls=%async_computation | async-start | bytes 393216 | tf_op jit(solution)/shard_map/all_to_all | solution.py:134
  277.1 10.3 %all-to-all-done = f32[32,2,6,128]{3,1,2,0:T(2,128)S(1)} async-done(((f32[32,2,6,128]{3,1,2,0:T(2,128)}), f32[32,2,6,128]{3,1,2,0:T(2,128)S(1)}, u32[]{:S(2)}, u32[]{:S(2)}) %all-to-all-start) | async-done | bytes 196640 | tf_op jit(solution)/shard_map/all_to_all | solution.py:134
  290.3 4.4 collective-permute-done.2
  294.7 15.3 %while.73 = (s32[]{:T(128)}, f32[4,8,6,128]{3,1,2,0:T(8,128)S(1)}, f32[4,8,6,128]{3,1,0,2:T(8,128)S(1)}, f32[4,8,7,128]{3,1,2,0:T(8,128)S(1)}, f32[4,8,7,128]{3,1,0,2:T(8,128)S(1)}, /*index=5*/s32[]{:T(128)}) while((s32[]{:T(128)}, f32[4,8,6,128]{3,1,2,0:T(8,128)S(1)}, f32[4,8,6,128]{3,1,0,2:T(8,128)S(1)}, f32[4,8,7,128]{3,1,2,0:T(8,128)S(1)}, ...), condition=%wide.region_81.82_spmd, body=%wide.region_62.81_spmd.sunk | while | flops 14424064 | bytes 581717 | solution.py:103
  312.2 11.1 %while.72 = (s32[]{:T(128)}, f32[4,8,6,128]{3,1,2,0:T(8,128)S(1)}, f32[4,8,7,128]{3,1,2,0:T(8,128)S(1)}, s32[]{:T(128)}) while((s32[]{:T(128)}, f32[4,8,6,128]{3,1,2,0:T(8,128)S(1)}, f32[4,8,7,128]{3,1,2,0:T(8,128)S(1)}, s32[]{:T(128)}) %tuple.338), condition=%wide.region_61.62_spmd, body=%wide.region_51.61_spmd.sunk | while | flops 8653825 | bytes 290877 | solution.py:98
  323.4 47.0 %all-gather.5.cloned.1.call-done = f32[1024,7,128]{2,0,1:T(8,128)} async-done(((f32[32,7,128]{2,0,1:T(8,128)}), f32[1024,7,128]{2,0,1:T(8,128)}) %all-gather.5.cloned.1.call-update) | async-done | bytes 3670032 | tf_op jit(solution)/shard_map/all_gather | solution.py:95
  370.4 6.1 %copy.168 = f32[1024,7,128]{2,1,0:T(8,128)} copy(f32[1024,7,128]{2,0,1:T(8,128)} %all-gather.5.cloned.1.call-done) | data formatting | bytes 7340032 | tf_op jit(solution)/shard_map/all_gather | solution.py:95
  379.3 104.9 %while.75 = (s32[]{:T(128)}, f32[32,6,128]{2,0,1:T(8,128)S(1)}, f32[64,6,128]{2,0,1:T(8,128)S(1)}, s32[]{:T(128)}, s32[192]{0:T(256)S(1)}, /*index=5*/s32[]{:T(1...) while((s32[]{:T(128)}, f32[32,6,128]{2,0,1:T(8,128)S(1)}, ...), condition=%wide.region_101.102_spmd.clone, body=%wide.region_82.101_spmd.clone.sunk | while | flops 21579340 | bytes 1131159 | solution.py:131
  380.7 3.6 fusion.353
  387.2 3.6 fusion.353
  393.8 3.6 fusion.353
  400.3 3.6 fusion.353
  406.9 3.6 fusion.353
  413.5 3.6 fusion.353
  420.0 3.6 fusion.353
  426.6 3.6 fusion.353
  433.1 3.6 fusion.353
  439.7 3.6 fusion.353
  446.2 3.6 fusion.353
  452.8 3.6 fusion.353
  459.4 3.6 fusion.353
  465.9 3.6 fusion.353
  472.5 3.6 fusion.353
  479.0 3.6 fusion.353
  484.4 68.2 %all_to_all.10 = f32[32,2,6,128]{3,1,2,0:T(2,128)S(1)} all-to-all(f32[32,2,6,128]{3,1,2,0:T(2,128)S(1)} %copy.170), channel_id=1, replica_groups=mesh['stream'=16,'cell'=32] {'cell'}, dimensions={0} | all-to-all | bytes 393216 | tf_op jit(solution)/shard_map/all_to_all | solution.py:134
  (1015 shorter events, 221.7 us)
Async XLA Ops:
  7.2 21.6 %copy-start.6 = (s32[1,1,32,2]{2,3,1,0:T(2,128)S(1)}, s32[1,1,32,2]{2,3,1,0:T(2,128)}, u32[]{:S(2)}) copy-start(s32[1,1,32,2]{2,3,1,0:T(2,128)} %param.22) | copy-start | bytes 772
  7.2 97.2 %all-gather.3.cloned.1.call-start = ((), (), s32[]{:S(2)}) async-start(), calls=%async_computation.2 | async-start | bytes 3784704 | tf_op jit(solution)/shard_map/all_gather | solution.py:95
  10.3 1.9 copy-start
  10.3 68.4 %collective-permute-start = (f32[32,7,128]{2,0,1:T(8,128)S(1)}, f32[32,7,128]{2,0,1:T(8,128)S(1)}, u32[]{:S(2)}, u32[]{:S(2)}) collective-permute-start(f32[32,7,128]{2,0,1:T(8,128)S(1)} %pad_maximum_fusion.1), channel_id=1, source_target_pairs={{0,32},{32,64},{64,96},{96,128},{128,160},{160,192},{192,224},{224... | collective-permute-start | bytes 344072 | tf_op jit(solution)/shard_map/ppermute | solution.py:18
  94.1 4.1 collective-permute-start.1
  98.3 15.1 %copy-start.4 = (s32[1,192]{1,0:T(1,128)S(1)}, s32[1,192]{1,0:T(1,128)}, u32[]{:S(2)}) copy-start(s32[1,192]{1,0:T(1,128)} %param.23) | copy-start | bytes 2308
  98.3 15.1 %copy-start.5 = (s32[1,192]{1,0:T(1,128)S(1)}, s32[1,192]{1,0:T(1,128)}, u32[]{:S(2)}) copy-start(s32[1,192]{1,0:T(1,128)} %param.24) | copy-start | bytes 2308
  113.3 174.3 %copy-start.2 = (f32[1,32,3,128]{3,1,2,0:T(8,128)S(1)}, f32[1,32,3,128]{3,1,2,0:T(8,128)}, u32[]{:S(2)}) copy-start(f32[1,32,3,128]{3,1,2,0:T(8,128)} %param.20) | copy-start | bytes 147460
  113.3 174.3 %copy-start.3 = (f32[1,32,3,128]{3,1,2,0:T(8,128)S(1)}, f32[1,32,3,128]{3,1,2,0:T(8,128)}, u32[]{:S(2)}) copy-start(f32[1,32,3,128]{3,1,2,0:T(8,128)} %param.19) | copy-start | bytes 147460
  219.0 68.4 %all-to-all-start = ((f32[32,2,6,128]{3,1,2,0:T(2,128)}), f32[32,2,6,128]{3,1,2,0:T(2,128)S(1)}, u32[]{:S(2)}, u32[]{:S(2)}) async-start(f32[32,2,6,128]{3,1,2,0:T(2,128)} %copy.160), calls=%async_computation | async-start | bytes 393216 | tf_op jit(solution)/shard_map/all_to_all | solution.py:134
  276.8 93.6 %all-gather.5.cloned.1.call-start = ((), (), s32[]{:S(2)}) async-start(), calls=%async_computation.3 | async-start | bytes 3784704 | tf_op jit(solution)/shard_map/all_gather | solution.py:95
  288.4 6.3 %collective-permute-start.2 = (f32[32,7,128]{2,0,1:T(8,128)}, f32[32,7,128]{2,0,1:T(8,128)S(1)}, u32[]{:S(2)}, u32[]{:S(2)}) collective-permute-start(f32[32,7,128]{2,0,1:T(8,128)} %pad_maximum_fusion), channel_id=1, source_target_pairs={{0,32},{32,64},{64,96},{96,128},{128,160},{160,192},{192,224},{224... | collective-permute-start | bytes 344072 | tf_op jit(solution)/shard_map/ppermute | solution.py:18
  294.7 28.6 %copy-start.1 = (f32[32,7,128]{2,0,1:T(8,128)S(1)}, f32[32,7,128]{2,0,1:T(8,128)}, u32[]{:S(2)}) copy-start(f32[32,7,128]{2,0,1:T(8,128)} %pad_maximum_fusion) | copy-start | bytes 344068
  310.1 13.3 %collective-permute-start.3 = (f32[32,6,128]{2,0,1:T(8,128)S(1)}, f32[32,6,128]{2,0,1:T(8,128)S(1)}, u32[]{:S(2)}, u32[]{:S(2)}) collective-permute-start(f32[32,6,128]{2,0,1:T(8,128)S(1)} %bitcast.595), channel_id=1, source_target_pairs={{32,0},{64,32},{96,64},{128,96},{160,128},{192,160},{224,192},{256... | collective-permute-start | bytes 294920 | tf_op jit(solution)/shard_map/ppermute | solution.py:18
Sparse Core Ops, SparseCore 0:
  12.4 91.9 all-gather.2
  288.5 81.8 all-gather.4
where the time goes:
time: 561 us; the launch traced here: 560 us
  other arithmetic  198 us (35%)
  blocking collectives  117 us (21%)
  waiting for transfers between devices  70 us (12%)
  starting transfers between devices  65.8 us (12%)
  local copies, waits for them, and re-layouts  59.3 us (11%)
  matrix products  27.2 us (5%)
  between operations  15.1 us (3%)
  loops' own time  7.65 us (1%)
    reduce_sum x40, other arithmetic, pair_terms(): jnp.sum(-cubic * twist[k] - 3.0 * quintic * dot_there * cross_here[k], ax...  143 us
    all_to_all x1, blocking collectives, rate(): lax.all_to_all(gained.reshape(owners, per_owner, 6, width), 'cell', split...  68.2 us
    all_to_all x1, starting transfers between devices, rate(): lax.all_to_all(gained.reshape(owners, per_owner, 6, width), 'cell', split...  57.8 us
    all_gather x2, waiting for transfers between devices, rate(): slab = lax.all_gather(packed, 'cell', axis=0, tiled=True)  53.1 us
    all_gather x1, blocking collectives, local(): lists = lax.all_gather(export_cells, 'cell', axis=1, tiled=True)  49 us
    gather x64, local copies, waits for them, and re-layouts, advance(): near, far = pair_terms(packed[ids_here], imported[ids_there], True)  35.5 us
    reduce_sum x8, other arithmetic, pair_terms(): jnp.sum(cubic * twist[k] - 3.0 * quintic * dot_here * cross_there[k], axi...  21 us
    convert_element_type x32, other arithmetic, advance(): (offset + jnp.arange(8, dtype=jnp.int32) < count).astype(jnp.float32)  20.8 us
  transfers between devices with their start and end apart: 7, of which 5 were waited for; matrix products, arithmetic and copies ran while one was open for 10% of the time, Pallas kernels for 0%

commit v1 on v0

v1 whole, which is shorter than its diff:
```python
import math

import jax
import jax.numpy as jnp
from jax import lax
from jax.experimental import pallas as pl
from jax.experimental.pallas import tpu as pltpu
from jax.sharding import PartitionSpec as P

sigma_sq = 0.09
spread_inv = 3.125
viscous = 0.01
time_step = 0.2
kernel_scale = 1.0 / (4.0 * math.pi)
smooth_rate = -spread_inv * math.log2(math.e)
smooth_scale = viscous * math.exp(spread_inv * sigma_sq)

f32 = jnp.float32
bf16 = jnp.bfloat16
MOMENTS = 48
NN = (((1,), (0,)), ((), ()))
NT = (((1,), (1,)), ((), ()))


def shifted(value, axis, steps):
    count = lax.axis_size(axis)
    leading, last = (max(0, -steps), min(count, count - steps))
    return lax.ppermute(value, axis, [(source, source + steps) for source in range(leading, last)])


def cross_rows(x, a):
    return [
        x[1] * a[2] - x[2] * a[1],
        x[2] * a[0] - x[0] * a[2],
        x[0] * a[1] - x[1] * a[0],
    ]


def rows_of(tile, first, count=3):
    return [tile[first + k : first + k + 1] for k in range(count)]


def split3(value):
    high = value.astype(bf16)
    rest = value - high.astype(f32)
    middle = rest.astype(bf16)
    low = (rest - middle.astype(f32)).astype(bf16)
    return high, middle, low


def split2(value):
    high = value.astype(bf16)
    return high, (value - high.astype(f32)).astype(bf16)


def features(tile):
    x, a = rows_of(tile, 0), rows_of(tile, 3)
    base = jnp.concatenate([tile[3:6]] + cross_rows(x, a) + [tile[6:8]], axis=0)
    full = jnp.concatenate([base, x[0] * base, x[1] * base, x[2] * base], axis=0)
    wide = jnp.concatenate(split3(full), axis=0)
    parts = [part.astype(f32) for part in split3(base)]
    narrow = jnp.concatenate(parts + [jnp.zeros((8, 128), f32)], axis=0).astype(bf16)
    return wide, narrow


def columns(tile):
    flipped = jnp.concatenate([tile] * 16, axis=0).T
    return [jnp.broadcast_to(flipped[:, k : k + 1], (128, 128)) for k in range(3)]


def weights(cols, tile):
    d = [cols[k] - tile[k : k + 1] for k in range(3)]
    soft = d[0] * d[0] + d[1] * d[1] + d[2] * d[2] + sigma_sq
    inverse = lax.rsqrt(soft)
    square = inverse * inverse
    cubic = square * inverse
    quintic = cubic * square
    smooth = jnp.exp2(soft * smooth_rate).astype(bf16)
    return split2(quintic), split2(cubic), smooth


def moments(wide, narrow, mats, dims):
    (qh, ql), (ch, cl), smooth = mats
    side = 1 if dims is NT else 0

    def dot(left, right):
        return lax.dot_general(left, right, dims, preferred_element_type=f32)

    out_q = dot(jnp.concatenate([wide, wide], axis=1), jnp.concatenate([qh, ql], axis=side))
    out_c = dot(jnp.concatenate([narrow, narrow], axis=1), jnp.concatenate([ch, cl], axis=side))
    out_s = dot(narrow, smooth)
    return jnp.concatenate(
        [
            out_q[0:32] + out_q[32:64] + out_q[64:96],
            out_c[0:8] + out_c[8:16] + out_c[16:24],
            out_s[0:8] + out_s[8:16] + out_s[16:24],
        ],
        axis=0,
    )


def credit(tile, mom):
    x, a = rows_of(tile, 0), rows_of(tile, 3)
    dot = a[0] * x[0] + a[1] * x[1] + a[2] * x[2]
    mixed = dot * mom[0:8] - a[0] * mom[8:16] - a[1] * mom[16:24] - a[2] * mom[24:32]
    turn = cross_rows(x, rows_of(mixed, 0))
    stretch = [turn[k] - mixed[3 + k : 4 + k] for k in range(3)]
    drift = cross_rows(x, rows_of(mom, 32))
    twist = cross_rows(a, rows_of(mom, 32))
    rows = [-kernel_scale * (drift[k] - mom[35 + k : 36 + k]) for k in range(3)]
    rows += [
        -kernel_scale * (twist[k] - 3.0 * stretch[k])
        + smooth_scale * (mom[40 + k : 41 + k] - a[k] * mom[46:47])
        for k in range(3)
    ]
    return jnp.concatenate(rows + [jnp.zeros((2, 128), f32)], axis=0)


def unrolled(count, step, body):
    def trip(t, carry):
        for u in range(step):
            body(t * step + u)
        return carry

    lax.fori_loop(0, count // step, trip, 0)


def pack_kernel(fill, exports, places, vortices, cells_ref, sent_ref):
    lane = lax.broadcasted_iota(jnp.int32, (1, 128), 1)
    for c in range(cells_ref.shape[0]):
        mask = (lane < fill[c]).astype(f32)
        rows = [places[k, c : c + 1] - 1.0 for k in range(3)]
        rows += [vortices[k, c : c + 1] * mask for k in range(3)]
        cells_ref[c] = jnp.concatenate(rows + [mask, jnp.zeros((1, 128), f32)], axis=0)

    def send(n):
        sent_ref[n] = cells_ref[exports[n]]

    unrolled(sent_ref.shape[0], 8, send)


def stream_kernel(cells_ref, above_ref, near_ref, far_ref):
    def pair(c):
        here, there = cells_ref[c], above_ref[c]
        mats = weights(columns(here), there)
        near_ref[c] = credit(here, moments(*features(there), mats, NT))
        far_ref[c] = credit(there, moments(*features(here), mats, NN))

    unrolled(cells_ref.shape[0], 4, pair)


def self_kernel(cells_ref, own_ref):
    def cell(c):
        here = cells_ref[c]
        own_ref[c] = credit(here, moments(*features(here), weights(columns(here), here), NN))

    unrolled(cells_ref.shape[0], 4, cell)


def remote_kernel(
    here_ids, there_ids, count, cells_ref, got_ref, near_ref, far_ref,
    cols, wide_here, narrow_here, wide_there, narrow_there, mom_here, mom_there,
):
    cells, imports = cells_ref.shape[0], got_ref.shape[0]
    blank = jnp.zeros((MOMENTS, 128), f32)

    def prepare_here(c):
        tile = cells_ref[c]
        wide_here[c], narrow_here[c] = features(tile)
        for k, col in enumerate(columns(tile)):
            cols[c, k] = col
        mom_here[c] = blank

    unrolled(cells, 4, prepare_here)

    def prepare_there(c):
        wide_there[c], narrow_there[c] = features(got_ref[c])
        mom_there[c] = blank

    unrolled(imports, 4, prepare_there)

    def pair(n):
        c, b = here_ids[n], there_ids[n]
        keep = jnp.minimum(b, imports - 1)
        own = jnp.minimum(c, cells - 1)
        mats = weights([cols[own, k] for k in range(3)], got_ref[keep])
        mom_here[c] += moments(wide_there[keep], narrow_there[keep], mats, NT)
        mom_there[b] += moments(wide_here[own], narrow_here[own], mats, NN)

    def trip(t, carry):
        for u in range(4):
            pair(t * 4 + u)
        return carry

    lax.fori_loop(0, (count[0] + 3) // 4, trip, 0)

    def finish_here(c):
        near_ref[c] = credit(cells_ref[c], mom_here[c])

    unrolled(cells, 4, finish_here)

    def finish_there(c):
        far_ref[c] = credit(got_ref[c], mom_there[c])

    unrolled(imports, 4, finish_there)


def gather_rates(exports, cells_ref, parts, back_ref, total_ref):
    total_ref[...] = parts[0][...] + parts[1][...] + parts[2][...] + parts[3][...]

    def add(n):
        total_ref[exports[n]] += back_ref[n]

    unrolled(back_ref.shape[0], 8, add)
    total_ref[...] = total_ref[...] * cells_ref[:, 6:7, :]


def middle_kernel(exports, cells_ref, own, near, remote, below, back_ref, first_ref, mid_ref, sent_ref):
    gather_rates(exports, cells_ref, (own, near, remote, below), back_ref, first_ref)
    mid_ref[...] = cells_ref[...] + time_step * first_ref[...]

    def send(n):
        sent_ref[n] = mid_ref[exports[n]]

    unrolled(sent_ref.shape[0], 8, send)


def last_kernel(
    exports, cells_ref, own, near, remote, below, back_ref, first_ref, places, vortices,
    new_places, new_vortices, total_ref,
):
    gather_rates(exports, cells_ref, (own, near, remote, below), back_ref, total_ref)
    half = 0.5 * time_step
    for c in range(cells_ref.shape[0]):
        change = half * (first_ref[c] + total_ref[c])
        for k in range(3):
            new_places[k, c : c + 1] = places[k, c : c + 1] + change[k : k + 1]
            new_vortices[k, c : c + 1] = vortices[k, c : c + 1] + change[3 + k : 4 + k]


def call(body, scalars, arrays, outs, scratch=(), name=None):
    whole = pl.BlockSpec(memory_space=pltpu.VMEM)
    single = len(outs) == 1
    shapes = [jax.ShapeDtypeStruct(shape, f32) for shape in outs]
    return pl.pallas_call(
        body,
        grid_spec=pltpu.PrefetchScalarGridSpec(
            num_scalar_prefetch=len(scalars),
            grid=(),
            in_specs=[whole] * len(arrays),
            out_specs=whole if single else [whole] * len(outs),
            scratch_shapes=list(scratch),
        ),
        out_shape=shapes[0] if single else shapes,
        compiler_params=pltpu.CompilerParams(vmem_limit_bytes=40 << 20),
        name=name,
    )(*scalars, *arrays)


def local(positions, strengths, fill, export_cells, pair_local, pair_remote, pair_count):
    places = jnp.transpose(positions[0], (1, 0, 2))
    vortices = jnp.transpose(strengths[0], (1, 0, 2))
    cells = places.shape[1]
    owners, per_owner = export_cells.shape[2:]
    imports = owners * per_owner
    exports = export_cells[0, 0].reshape(-1)
    slots = pair_local.shape[1]
    count = pair_count[0]
    alive = jnp.arange(slots, dtype=jnp.int32) < count
    here_ids = jnp.where(alive, pair_local[0], cells)
    there_ids = jnp.where(alive, pair_remote[0], imports)
    tile, traded = (cells, 8, 128), (imports, 8, 128)

    def exchange(value):
        value = value.reshape(owners, per_owner, 8, 128)
        value = lax.all_to_all(value, "cell", split_axis=0, concat_axis=0, tiled=True)
        return value.reshape(traded)

    def rates(packed, sent):
        above = shifted(packed, "stream", 1)
        got = exchange(sent)
        near, far = call(stream_kernel, (), (packed, above), (tile, tile), name="stream")
        below = shifted(far, "stream", -1)
        got, near = lax.optimization_barrier((got, near))
        remote, back = call(
            remote_kernel, (here_ids, there_ids, count), (packed, got), (tile, traded),
            (
                pltpu.VMEM((cells, 3, 128, 128), f32),
                pltpu.VMEM((cells, 96, 128), bf16),
                pltpu.VMEM((cells, 32, 128), bf16),
                pltpu.VMEM((imports, 96, 128), bf16),
                pltpu.VMEM((imports, 32, 128), bf16),
                pltpu.VMEM((cells + 1, MOMENTS, 128), f32),
                pltpu.VMEM((imports + 1, MOMENTS, 128), f32),
            ),
            name="remote",
        )
        late, _ = lax.optimization_barrier((packed, back))
        back = exchange(back)
        own = call(self_kernel, (), (late,), (tile,), name="own")
        return own, near, remote, below, back

    packed, sent = call(pack_kernel, (fill[0], exports), (places, vortices), (tile, traded), name="pack")
    first, middle, sent = call(
        middle_kernel, (exports,), (packed, *rates(packed, sent)), (tile, tile, traded), name="middle"
    )
    shape = places.shape
    new_places, new_vortices = call(
        last_kernel, (exports,), (middle, *rates(middle, sent), first, places, vortices), (shape, shape),
        (pltpu.VMEM(tile, f32),), name="last",
    )
    return (jnp.transpose(new_places, (1, 0, 2))[None], jnp.transpose(new_vortices, (1, 0, 2))[None])


def solution(mesh):
    in_specs = (
        P("stream", "cell", None, None),
        P("stream", "cell", None, None),
        P("stream", "cell"),
        P("stream", "cell", None, None),
        P("stream", "cell"),
        P("stream", "cell"),
        P("stream", "cell"),
    )
    out_specs = (P("stream", "cell", None, None), P("stream", "cell", None, None))
    return jax.shard_map(local, mesh=mesh, in_specs=in_specs, out_specs=out_specs, check_vma=False)
```

time: 561 us -> 161 us (0.29)
  the two profiles are of different devices: /device:TPU:8 before, /device:TPU:24 now
where the time goes in v1:
time: 161 us; the launch traced here: 160 us
  Pallas kernels  91.5 us (57%)
  starting transfers between devices  45 us (28%)
  waiting for transfers between devices  18.5 us (11%)
  local copies, waits for them, and re-layouts  3.79 us (2%)
    pallas_call x9, Pallas kernels, call(): pl.pallas_call(body, grid_spec=pltpu.PrefetchScalarGridSpec(num_scalar_pr...  91.5 us
    all_to_all x4, starting transfers between devices, exchange(): lax.all_to_all(value, 'cell', split_axis=0, concat_axis=0, tiled=True)  37.2 us
    all_to_all x4, waiting for transfers between devices, exchange(): lax.all_to_all(value, 'cell', split_axis=0, concat_axis=0, tiled=True)  11.1 us
    ppermute x4, starting transfers between devices, shifted(): lax.ppermute(value, axis, [(source, source + steps) for source in range(l...  7.81 us
    ppermute x4, waiting for transfers between devices, shifted(): lax.ppermute(value, axis, [(source, source + steps) for source in range(l...  7.39 us
    unnamed x15, local copies, waits for them, and re-layouts  3.69 us
  transfers between devices with their start and end apart: 8, of which 4 were waited for; matrix products, arithmetic and copies ran while one was open for 0% of the time, Pallas kernels for 15%

profile of v1, /device:TPU:24, one launch (start us, length us, event | category | flops | bytes accessed | tf_op | source)
XLA Modules:
  0.0 160.2 jit_solution(6854612633647838440)
XLA Ops:
  0.6 0.8 copy.10
  1.4 0.1 reshape_squeeze.3.exports
  1.5 0.0 copy-start.4
  1.5 0.6 copy-done.4
  2.2 0.8 copy-done
  3.0 0.8 copy-done.2
  3.8 1.4 pack.1
  5.2 13.2 %all-to-all-start = ((f32[32,2,8,128]{3,2,1,0:T(8,128)}), f32[32,2,8,128]{3,2,1,0:T(8,128)S(1)}, u32[]{:S(2)}, u32[]{:S(2)}) async-start(f32[32,2,8,128]{3,2,1,0:T(8,128)} %bitcast.9), calls=%async_computation | async-start | bytes 524288 | tf_op jit(solution)/shard_map/all_to_all | solution.py:276
  18.4 0.0 copy-start.6
  18.4 1.9 %collective-permute-start = (f32[32,8,128]{2,1,0:T(8,128)S(1)}, f32[32,8,128]{2,1,0:T(8,128)S(1)}, u32[]{:S(2)}, u32[]{:S(2)}) collective-permute-start(f32[32,8,128]{2,1,0:T(8,128)S(1)} %get-tuple-element.28.cells_ref), channel_id=1, source_target_pairs={{0,32},{32,64},{64,96},{96,128},{128,160},{160,192},{192,224},{224... | collective-permute-start | bytes 393224 | tf_op jit(solution)/shard_map/ppermute | solution.py:28
  21.0 0.0 copy-start.5
  21.0 0.7 copy-done.5
  21.6 3.0 %collective-permute-done.above_ref = f32[32,8,128]{2,1,0:T(8,128)S(1)} collective-permute-done((f32[32,8,128]{2,1,0:T(8,128)S(1)}, f32[32,8,128]{2,1,0:T(8,128)S(1)}, u32[]{:S(2)}, u32[]{:S(2)}) %collective-permute-start) | collective-permute-done | bytes 131104 | tf_op jit(solution)/shard_map/ppermute | solution.py:28
  24.7 6.9 %stream.2 = (f32[32,8,128]{2,1,0:T(8,128)S(1)}, f32[32,8,128]{2,1,0:T(8,128)S(1)}) custom-call(f32[32,8,128]{2,1,0:T(8,128)S(1)} %get-tuple-element.28.cells_ref, f32[32,8,128]{2,1,0:T(8,128)S(1)} %collective-permute-done.above_ref), custom_call_target="tpu_custom_call" | custom-call | tf_op jit(solution)/shard_map/stream/pallas_call | solution.py:245
  31.6 31.5 %remote.2 = (f32[32,8,128]{2,1,0:T(8,128)S(1)}, f32[64,8,128]{2,1,0:T(8,128)}) custom-call(s32[192]{0:T(256)S(1)} %get-tuple-element.45.here_ids, s32[192]{0:T(256)S(1)} %get-tuple-element.44.there_ids, s32[1]{0:T(128)} %bitcast.28.count, f32[32,8,128]{2,1,0:T(8,128)S(1)} %get-tuple-element.28.cells_ref, f32[64,8,128]{2,1,0:T(8,128)S(1)} %bitcast.31), custom_call_target="tpu_custom_call" | custom-call | tf_op jit(solution)/shard_map/remote/pallas_call | solution.py:245
  63.1 9.8 %all-to-all-start.1 = ((f32[32,2,8,128]{3,2,1,0:T(8,128)}), f32[32,2,8,128]{3,2,1,0:T(8,128)S(1)}, u32[]{:S(2)}, u32[]{:S(2)}) async-start(f32[32,2,8,128]{3,2,1,0:T(8,128)} %bitcast.11), calls=%async_computation.1 | async-start | bytes 524288 | tf_op jit(solution)/shard_map/all_to_all | solution.py:276
  72.9 1.9 %collective-permute-start.1 = (f32[32,8,128]{2,1,0:T(8,128)S(1)}, f32[32,8,128]{2,1,0:T(8,128)S(1)}, u32[]{:S(2)}, u32[]{:S(2)}) collective-permute-start(f32[32,8,128]{2,1,0:T(8,128)S(1)} %get-tuple-element.31), channel_id=1, source_target_pairs={{32,0},{64,32},{96,64},{128,96},{160,128},{192,160},{224,192},{256... | collective-permute-start | bytes 393224 | tf_op jit(solution)/shard_map/ppermute | solution.py:28
  74.8 5.0 %own.2 = f32[32,8,128]{2,1,0:T(8,128)S(1)} custom-call(f32[32,8,128]{2,1,0:T(8,128)S(1)} %get-tuple-element.28.cells_ref), custom_call_target="tpu_custom_call" | custom-call | tf_op jit(solution)/shard_map/own/pallas_call | solution.py:245
  79.9 5.8 %all-to-all-done.1 = f32[32,2,8,128]{3,2,1,0:T(8,128)S(1)} async-done(((f32[32,2,8,128]{3,2,1,0:T(8,128)}), f32[32,2,8,128]{3,2,1,0:T(8,128)S(1)}, u32[]{:S(2)}, u32[]{:S(2)}) %all-to-all-start.1) | async-done | bytes 262176 | tf_op jit(solution)/shard_map/all_to_all | solution.py:276
  85.7 1.6 middle.1
  87.3 4.4 %all-to-all-start.2 = ((f32[32,2,8,128]{3,2,1,0:T(8,128)}), f32[32,2,8,128]{3,2,1,0:T(8,128)S(1)}, u32[]{:S(2)}, u32[]{:S(2)}) async-start(f32[32,2,8,128]{3,2,1,0:T(8,128)} %bitcast.13), calls=%async_computation.2 | async-start | bytes 524288 | tf_op jit(solution)/shard_map/all_to_all | solution.py:276
  91.7 1.9 %collective-permute-start.2 = (f32[32,8,128]{2,1,0:T(8,128)S(1)}, f32[32,8,128]{2,1,0:T(8,128)S(1)}, u32[]{:S(2)}, u32[]{:S(2)}) collective-permute-start(f32[32,8,128]{2,1,0:T(8,128)S(1)} %get-tuple-element.37.cells_ref), channel_id=1, source_target_pairs={{0,32},{32,64},{64,96},{96,128},{128,160},{160,192},{192,224},{224... | collective-permute-start | bytes 393224 | tf_op jit(solution)/shard_map/ppermute | solution.py:28
  93.6 4.4 %collective-permute-done.2.above_ref = f32[32,8,128]{2,1,0:T(8,128)S(1)} collective-permute-done((f32[32,8,128]{2,1,0:T(8,128)S(1)}, f32[32,8,128]{2,1,0:T(8,128)S(1)}, u32[]{:S(2)}, u32[]{:S(2)}) %collective-permute-start.2) | collective-permute-done | bytes 131104 | tf_op jit(solution)/shard_map/ppermute | solution.py:28
  98.0 6.9 %stream.3 = (f32[32,8,128]{2,1,0:T(8,128)S(1)}, f32[32,8,128]{2,1,0:T(8,128)S(1)}) custom-call(f32[32,8,128]{2,1,0:T(8,128)S(1)} %get-tuple-element.37.cells_ref, f32[32,8,128]{2,1,0:T(8,128)S(1)} %collective-permute-done.2.above_ref), custom_call_target="tpu_custom_call" | custom-call | tf_op jit(solution)/shard_map/stream/pallas_call | solution.py:245
  104.9 31.5 %remote.3 = (f32[32,8,128]{2,1,0:T(8,128)S(1)}, f32[64,8,128]{2,1,0:T(8,128)}) custom-call(s32[192]{0:T(256)S(1)} %get-tuple-element.45.here_ids, s32[192]{0:T(256)S(1)} %get-tuple-element.44.there_ids, s32[1]{0:T(128)} %bitcast.29.count, f32[32,8,128]{2,1,0:T(8,128)S(1)} %get-tuple-element.37.cells_ref, f32[64,8,128]{2,1,0:T(8,128)S(1)} %bitcast.32), custom_call_target="tpu_custom_call" | custom-call | tf_op jit(solution)/shard_map/remote/pallas_call | solution.py:245
  136.4 9.8 %all-to-all-start.3 = ((f32[32,2,8,128]{3,2,1,0:T(8,128)}), f32[32,2,8,128]{3,2,1,0:T(8,128)S(1)}, u32[]{:S(2)}, u32[]{:S(2)}) async-start(f32[32,2,8,128]{3,2,1,0:T(8,128)} %bitcast.15), calls=%async_computation.3 | async-start | bytes 524288 | tf_op jit(solution)/shard_map/all_to_all | solution.py:276
  146.2 0.0 copy-start.1
  146.2 0.0 copy-start.3
  146.3 2.1 %collective-permute-start.3 = (f32[32,8,128]{2,1,0:T(8,128)S(1)}, f32[32,8,128]{2,1,0:T(8,128)S(1)}, u32[]{:S(2)}, u32[]{:S(2)}) collective-permute-start(f32[32,8,128]{2,1,0:T(8,128)S(1)} %get-tuple-element.40), channel_id=1, source_target_pairs={{32,0},{64,32},{96,64},{128,96},{160,128},{192,160},{224,192},{256... | collective-permute-start | bytes 393224 | tf_op jit(solution)/shard_map/ppermute | solution.py:28
  148.3 5.0 %own.3 = f32[32,8,128]{2,1,0:T(8,128)S(1)} custom-call(f32[32,8,128]{2,1,0:T(8,128)S(1)} %get-tuple-element.37.cells_ref), custom_call_target="tpu_custom_call" | custom-call | tf_op jit(solution)/shard_map/own/pallas_call | solution.py:245
  153.4 5.3 %all-to-all-done.3 = f32[32,2,8,128]{3,2,1,0:T(8,128)S(1)} async-done(((f32[32,2,8,128]{3,2,1,0:T(8,128)}), f32[32,2,8,128]{3,2,1,0:T(8,128)S(1)}, u32[]{:S(2)}, u32[]{:S(2)}) %all-to-all-start.3) | async-done | bytes 262176 | tf_op jit(solution)/shard_map/all_to_all | solution.py:276
  158.7 1.5 last.1
  (10 shorter events, 0.0 us)
Async XLA Ops:
  1.5 0.7 copy-start.4
  2.2 0.8 copy-start
  3.0 0.8 copy-start.2
  5.2 26.4 %all-to-all-start = ((f32[32,2,8,128]{3,2,1,0:T(8,128)}), f32[32,2,8,128]{3,2,1,0:T(8,128)S(1)}, u32[]{:S(2)}, u32[]{:S(2)}) async-start(f32[32,2,8,128]{3,2,1,0:T(8,128)} %bitcast.9), calls=%async_computation | async-start | bytes 524288 | tf_op jit(solution)/shard_map/all_to_all | solution.py:276
  18.4 2.6 %copy-start.6 = (s32[1,192]{1,0:T(1,128)S(1)}, s32[1,192]{1,0:T(1,128)}, u32[]{:S(2)}) copy-start(s32[1,192]{1,0:T(1,128)} %param.11) | copy-start | bytes 2308
  18.4 6.3 %collective-permute-start = (f32[32,8,128]{2,1,0:T(8,128)S(1)}, f32[32,8,128]{2,1,0:T(8,128)S(1)}, u32[]{:S(2)}, u32[]{:S(2)}) collective-permute-start(f32[32,8,128]{2,1,0:T(8,128)S(1)} %get-tuple-element.28.cells_ref), channel_id=1, source_target_pairs={{0,32},{32,64},{64,96},{96,128},{128,160},{160,192},{192,224},{224... | collective-permute-start | bytes 393224 | tf_op jit(solution)/shard_map/ppermute | solution.py:28
  21.0 0.7 copy-start.5
  63.1 22.6 %all-to-all-start.1 = ((f32[32,2,8,128]{3,2,1,0:T(8,128)}), f32[32,2,8,128]{3,2,1,0:T(8,128)S(1)}, u32[]{:S(2)}, u32[]{:S(2)}) async-start(f32[32,2,8,128]{3,2,1,0:T(8,128)} %bitcast.11), calls=%async_computation.1 | async-start | bytes 524288 | tf_op jit(solution)/shard_map/all_to_all | solution.py:276
  72.9 7.0 %collective-permute-start.1 = (f32[32,8,128]{2,1,0:T(8,128)S(1)}, f32[32,8,128]{2,1,0:T(8,128)S(1)}, u32[]{:S(2)}, u32[]{:S(2)}) collective-permute-start(f32[32,8,128]{2,1,0:T(8,128)S(1)} %get-tuple-element.31), channel_id=1, source_target_pairs={{32,0},{64,32},{96,64},{128,96},{160,128},{192,160},{224,192},{256... | collective-permute-start | bytes 393224 | tf_op jit(solution)/shard_map/ppermute | solution.py:28
  87.3 17.6 %all-to-all-start.2 = ((f32[32,2,8,128]{3,2,1,0:T(8,128)}), f32[32,2,8,128]{3,2,1,0:T(8,128)S(1)}, u32[]{:S(2)}, u32[]{:S(2)}) async-start(f32[32,2,8,128]{3,2,1,0:T(8,128)} %bitcast.13), calls=%async_computation.2 | async-start | bytes 524288 | tf_op jit(solution)/shard_map/all_to_all | solution.py:276
  91.7 6.3 %collective-permute-start.2 = (f32[32,8,128]{2,1,0:T(8,128)S(1)}, f32[32,8,128]{2,1,0:T(8,128)S(1)}, u32[]{:S(2)}, u32[]{:S(2)}) collective-permute-start(f32[32,8,128]{2,1,0:T(8,128)S(1)} %get-tuple-element.37.cells_ref), channel_id=1, source_target_pairs={{0,32},{32,64},{64,96},{96,128},{128,160},{160,192},{192,224},{224... | collective-permute-start | bytes 393224 | tf_op jit(solution)/shard_map/ppermute | solution.py:28
  136.4 22.3 %all-to-all-start.3 = ((f32[32,2,8,128]{3,2,1,0:T(8,128)}), f32[32,2,8,128]{3,2,1,0:T(8,128)S(1)}, u32[]{:S(2)}, u32[]{:S(2)}) async-start(f32[32,2,8,128]{3,2,1,0:T(8,128)} %bitcast.15), calls=%async_computation.3 | async-start | bytes 524288 | tf_op jit(solution)/shard_map/all_to_all | solution.py:276
  146.2 12.5 %copy-start.1 = (f32[1,32,3,128]{3,1,2,0:T(8,128)S(1)}, f32[1,32,3,128]{3,1,2,0:T(8,128)}, u32[]{:S(2)}) copy-start(f32[1,32,3,128]{3,1,2,0:T(8,128)} %param.7) | copy-start | bytes 147460
  146.2 12.5 %copy-start.3 = (f32[1,32,3,128]{3,1,2,0:T(8,128)S(1)}, f32[1,32,3,128]{3,1,2,0:T(8,128)}, u32[]{:S(2)}) copy-start(f32[1,32,3,128]{3,1,2,0:T(8,128)} %param.8) | copy-start | bytes 147460
  146.3 7.1 %collective-permute-start.3 = (f32[32,8,128]{2,1,0:T(8,128)S(1)}, f32[32,8,128]{2,1,0:T(8,128)S(1)}, u32[]{:S(2)}, u32[]{:S(2)}) collective-permute-start(f32[32,8,128]{2,1,0:T(8,128)S(1)} %get-tuple-element.40), channel_id=1, source_target_pairs={{32,0},{64,32},{96,64},{128,96},{160,128},{192,160},{224,192},{256... | collective-permute-start | bytes 393224 | tf_op jit(solution)/shard_map/ppermute | solution.py:28

commit v2 on v1

v2 whole, which is shorter than its diff:
```python
import math

import jax
import jax.numpy as jnp
from jax import lax
from jax.experimental import pallas as pl
from jax.experimental.pallas import tpu as pltpu
from jax.sharding import PartitionSpec as P

sigma_sq = 0.09
spread_inv = 3.125
viscous = 0.01
time_step = 0.2
kernel_scale = 1.0 / (4.0 * math.pi)
smooth_rate = -spread_inv * math.log2(math.e)
smooth_scale = viscous * math.exp(spread_inv * sigma_sq)

f32 = jnp.float32
bf16 = jnp.bfloat16
MOMENTS = 48
NN = (((1,), (0,)), ((), ()))
NT = (((1,), (1,)), ((), ()))


def shifted(value, axis, steps):
    count = lax.axis_size(axis)
    leading, last = (max(0, -steps), min(count, count - steps))
    return lax.ppermute(value, axis, [(source, source + steps) for source in range(leading, last)])


def cross_rows(x, a):
    return [
        x[1] * a[2] - x[2] * a[1],
        x[2] * a[0] - x[0] * a[2],
        x[0] * a[1] - x[1] * a[0],
    ]


def dot_rows(x, a):
    return x[0] * a[0] + x[1] * a[1] + x[2] * a[2]


def unrolled(count, step, body):
    def trip(t, carry):
        for u in range(step):
            body(t * step + u)
        return carry

    lax.fori_loop(0, count // step, trip, 0)


def split2(value):
    high = value.astype(bf16)
    return high, (value - high.astype(f32)).astype(bf16)


def fill_bases(tiles, bases):
    bases[...] = tiles[...]

    def group(t):
        x, a = [[tiles[pl.ds(t * 64 + first + k, 8, stride=8), :] for k in range(3)] for first in (0, 3)]
        for k, row in enumerate(cross_rows(x, a)):
            bases[pl.ds(t * 64 + k, 8, stride=8), :] = row

    unrolled(tiles.shape[0] // 64, 2, group)


def features(tile, base):
    x = [tile[k : k + 1] for k in range(3)]
    parts = []
    for scale in (None, x[0], x[1], x[2], dot_rows(x, x)):
        value = base if scale is None else scale * base
        high = value.astype(bf16).astype(f32)
        rest = value - high
        middle = rest.astype(bf16).astype(f32)
        parts += [high, middle, rest - middle]
        if scale is None:
            parts.append(jnp.zeros((8, 128), f32))
    return jnp.concatenate(parts, axis=0).astype(bf16)


def columns(tile):
    flipped = jnp.concatenate([tile] * 16, axis=0).T
    return [jnp.broadcast_to(flipped[:, k : k + 1], (128, 128)) for k in range(3)]


def weights(cols, tile):
    d = [cols[k] - tile[k : k + 1] for k in range(3)]
    soft = dot_rows(d, d) + sigma_sq
    inverse = lax.rsqrt(soft)
    square = inverse * inverse
    quintic = square * square * inverse
    smooth = jnp.exp2(soft * smooth_rate)
    return split2(quintic), split2(smooth)


def moments(wide, mats, dims):
    side = 1 if dims is NT else 0
    twice = jnp.concatenate([wide, wide], axis=1)
    quintic, smooth = [jnp.concatenate(parts, axis=side) for parts in mats]
    q = lax.dot_general(twice, quintic, dims, preferred_element_type=f32)
    s = lax.dot_general(twice[0:32], smooth, dims, preferred_element_type=f32)
    starts = (0, 32, 56, 80, 104)
    tiles = [q[k : k + 8] + q[k + 8 : k + 16] + q[k + 16 : k + 24] for k in starts]
    return tiles + [s[0:8] + s[8:16] + s[16:24]]


def put(target, c, tiles, add=False):
    for k, tile in enumerate(tiles):
        rows = pl.ds(pl.multiple_of(c * MOMENTS + 8 * k, 8), 8)
        target[rows, :] = target[rows, :] + tile if add else tile


def credits(tiles, moment, out):
    def group(t):
        def cell_rows(first, count=3):
            return [tiles[pl.ds(t * 64 + first + k, 8, stride=8), :] for k in range(count)]

        def sums(which, first, count=3):
            at = t * 8 * MOMENTS + which * 8 + first
            return [moment[pl.ds(at + k, 8, stride=MOMENTS), :] for k in range(count)]

        x, a = cell_rows(0), cell_rows(3)
        spin, norm = dot_rows(a, x), dot_rows(x, x) + sigma_sq
        twice = [2.0 * x[k] for k in range(3)]
        parts = [sums(which, 0, 6) for which in range(5)]
        mixed = [
            spin * parts[0][r] - a[0] * parts[1][r] - a[1] * parts[2][r] - a[2] * parts[3][r] for r in range(6)
        ]
        cubic = [
            norm * parts[0][r] + parts[4][r]
            - twice[0] * parts[1][r] - twice[1] * parts[2][r] - twice[2] * parts[3][r]
            for r in range(6)
        ]
        turn, drift = cross_rows(x, mixed[3:6]), cross_rows(x, cubic[3:6])
        twist = cross_rows(a, cubic[3:6])
        spread, total = sums(5, 3), sums(5, 6, 1)[0]
        for k in range(3):
            out[pl.ds(t * 64 + k, 8, stride=8), :] = -kernel_scale * (drift[k] - cubic[k])
            out[pl.ds(t * 64 + 3 + k, 8, stride=8), :] = -kernel_scale * (
                twist[k] - 3.0 * (turn[k] - mixed[k])
            ) + smooth_scale * (spread[k] - a[k] * total)
        for k in (6, 7):
            out[pl.ds(t * 64 + k, 8, stride=8), :] = jnp.zeros((8, 128), f32)

    unrolled(tiles.shape[0] // 64, 2, group)


def tile_rows(ref, c):
    return ref[pl.ds(pl.multiple_of(c * 8, 8), 8), :]


def pack_kernel(fill, exports, places, vortices, cells_ref, sent_ref):
    lane = lax.broadcasted_iota(jnp.int32, (1, 128), 1)
    for c in range(cells_ref.shape[0] // 8):
        mask = (lane < fill[c]).astype(f32)
        rows = [places[k, c : c + 1] - 1.0 for k in range(3)]
        rows += [vortices[k, c : c + 1] * mask for k in range(3)]
        cells_ref[8 * c : 8 * c + 8] = jnp.concatenate(rows + [mask, jnp.zeros((1, 128), f32)], axis=0)
    send(exports, cells_ref, sent_ref)


def send(exports, cells_ref, sent_ref):
    def one(n):
        sent_ref[pl.ds(pl.multiple_of(n * 8, 8), 8), :] = tile_rows(cells_ref, exports[n])

    unrolled(sent_ref.shape[0] // 8, 8, one)


def near_kernel(
    cells_ref, above_ref, near_ref, far_ref, wide_ref, cols_out, base_here, base_there, mom_near, mom_far, kept, sem
):
    fill_bases(cells_ref, base_here)
    fill_bases(above_ref, base_there)

    def cell(c):
        here, there = tile_rows(cells_ref, c), tile_rows(above_ref, c)
        wide = features(here, tile_rows(base_here, c))
        wide_there = features(there, tile_rows(base_there, c))
        cols = columns(here)
        joint = weights(cols, there)
        near = moments(wide_there, joint, NT)
        far = moments(wide, joint, NN)
        own = moments(wide, weights(cols, here), NN)
        wide_ref[c] = wide
        for k in range(3):
            kept[c, k] = cols[k]
        put(mom_far, c, far)
        put(mom_near, c, [p + q for p, q in zip(near, own)])

    unrolled(wide_ref.shape[0], 4, cell)
    copy = pltpu.make_async_copy(kept, cols_out, sem)
    copy.start()
    credits(above_ref, mom_far, far_ref)
    credits(cells_ref, mom_near, near_ref)
    copy.wait()


def far_kernel(here_ids, there_ids, count, cols_ref, wide_ref, got_ref, far_ref, wide_out, cols, sem, base, mom):
    cells, imports = cols.shape[0], wide_out.shape[0]
    copy = pltpu.make_async_copy(cols_ref, cols, sem)
    copy.start()
    fill_bases(got_ref, base)
    mom[...] = jnp.zeros(mom.shape, f32)

    def prepare(b):
        wide_out[b] = features(tile_rows(got_ref, b), tile_rows(base, b))

    unrolled(imports, 8, prepare)
    copy.wait()

    def pair(n):
        c, b = jnp.minimum(here_ids[n], cells - 1), there_ids[n]
        mats = weights([cols[c, k] for k in range(3)], tile_rows(got_ref, jnp.minimum(b, imports - 1)))
        put(mom, b, moments(wide_ref[c], mats, NN), add=True)

    pairs(count, pair)
    credits(got_ref, mom, far_ref)


def here_kernel(here_ids, there_ids, count, cols_ref, wide_ref, got_ref, cells_ref, own_ref, cols, sem, mom):
    cells, imports = cols.shape[0], wide_ref.shape[0]
    copy = pltpu.make_async_copy(cols_ref, cols, sem)
    copy.start()
    mom[...] = jnp.zeros(mom.shape, f32)
    copy.wait()

    def pair(n):
        c, b = here_ids[n], jnp.minimum(there_ids[n], imports - 1)
        cell = jnp.minimum(c, cells - 1)
        mats = weights([cols[cell, k] for k in range(3)], tile_rows(got_ref, b))
        put(mom, c, moments(wide_ref[b], mats, NT), add=True)

    pairs(count, pair)
    credits(cells_ref, mom, own_ref)


def pairs(count, pair):
    def trip(t, carry):
        for u in range(16):
            pair(t * 16 + u)
        return carry

    lax.fori_loop(0, (count[0] + 15) // 16, trip, 0)


def gather_rates(exports, cells_ref, parts, back_ref, total_ref):
    total_ref[...] = parts[0][...] + parts[1][...] + parts[2][...]

    def add(n):
        at = pl.ds(pl.multiple_of(exports[n] * 8, 8), 8)
        total_ref[at, :] = total_ref[at, :] + tile_rows(back_ref, n)

    unrolled(back_ref.shape[0] // 8, 8, add)
    for c in range(total_ref.shape[0] // 8):
        rows = slice(8 * c, 8 * c + 8)
        total_ref[rows] = total_ref[rows] * cells_ref[8 * c + 6 : 8 * c + 7]


def middle_kernel(exports, cells_ref, near, remote, below, back_ref, first_ref, mid_ref, sent_ref):
    gather_rates(exports, cells_ref, (near, remote, below), back_ref, first_ref)
    mid_ref[...] = cells_ref[...] + time_step * first_ref[...]
    send(exports, mid_ref, sent_ref)


def last_kernel(
    exports, cells_ref, near, remote, below, back_ref, first_ref, places, vortices,
    new_places, new_vortices, total_ref,
):
    gather_rates(exports, cells_ref, (near, remote, below), back_ref, total_ref)
    half = 0.5 * time_step
    for c in range(total_ref.shape[0] // 8):
        change = half * (first_ref[8 * c : 8 * c + 8] + total_ref[8 * c : 8 * c + 8])
        for k in range(3):
            new_places[k, c : c + 1] = places[k, c : c + 1] + change[k : k + 1]
            new_vortices[k, c : c + 1] = vortices[k, c : c + 1] + change[3 + k : 4 + k]


def call(body, scalars, arrays, outs, scratch=(), name=None):
    def spec(shape):
        return pl.BlockSpec(memory_space=pltpu.HBM if len(shape) == 4 else pltpu.VMEM)

    def shape(out):
        if len(out) == 4:
            return pltpu.HBM(out, f32)
        return jax.ShapeDtypeStruct(out, bf16 if len(out) == 3 and out[1] == 128 else f32)

    outs = [shape(out) for out in outs]
    arrays = [pltpu.with_memory_space_constraint(one, pltpu.HBM) if one.ndim == 4 else one for one in arrays]
    return pl.pallas_call(
        body,
        grid_spec=pltpu.PrefetchScalarGridSpec(
            num_scalar_prefetch=len(scalars),
            grid=(),
            in_specs=[spec(array.shape) for array in arrays],
            out_specs=[spec(out.shape) for out in outs],
            scratch_shapes=[pltpu.VMEM(one, f32) if isinstance(one, tuple) else one for one in scratch],
        ),
        out_shape=outs,
        compiler_params=pltpu.CompilerParams(vmem_limit_bytes=20 << 20),
        name=name,
    )(*scalars, *arrays)


def local(positions, strengths, fill, export_cells, pair_local, pair_remote, pair_count):
    places = jnp.transpose(positions[0], (1, 0, 2))
    vortices = jnp.transpose(strengths[0], (1, 0, 2))
    cells = places.shape[1]
    owners, per_owner = export_cells.shape[2:]
    imports = owners * per_owner
    exports = export_cells[0, 0].reshape(-1)
    count = pair_count[0]
    alive = jnp.arange(pair_local.shape[1], dtype=jnp.int32) < count
    here_ids = jnp.where(alive, pair_local[0], cells)
    there_ids = jnp.where(alive, pair_remote[0], imports)
    tile, traded = (cells * 8, 128), (imports * 8, 128)
    spread, done = (cells, 3, 128, 128), pltpu.SemaphoreType.DMA

    def exchange(value):
        value = value.reshape(owners, per_owner, 8, 128)
        value = lax.all_to_all(value, "cell", split_axis=0, concat_axis=0, tiled=True)
        return value.reshape(traded)

    def rates(packed, sent):
        above = shifted(packed, "stream", 1)
        got = exchange(sent)
        near, far, wide, cols = call(
            near_kernel, (), (packed, above),
            (tile, tile, (cells, 128, 128), spread),
            (tile, tile, (cells * MOMENTS, 128), (cells * MOMENTS, 128), spread, done), name="near",
        )
        below = shifted(far, "stream", -1)
        got, near = lax.optimization_barrier((got, near))
        listed = (here_ids, there_ids, count)
        back, wide_there = call(
            far_kernel, listed, (cols, wide, got), (traded, (imports, 128, 128)),
            (spread, done, traded, ((imports + 1) * MOMENTS, 128)), name="far",
        )
        returned = exchange(back)
        (remote,) = call(
            here_kernel, listed, (cols, wide_there, got, packed), (tile,),
            (spread, done, ((cells + 1) * MOMENTS, 128),), name="here",
        )
        return near, remote, below, returned

    packed, sent = call(pack_kernel, (fill[0], exports), (places, vortices), (tile, traded), name="pack")
    first, middle, sent = call(
        middle_kernel, (exports,), (packed, *rates(packed, sent)), (tile, tile, traded), name="middle"
    )
    shape = places.shape
    new_places, new_vortices = call(
        last_kernel, (exports,), (middle, *rates(middle, sent), first, places, vortices), (shape, shape),
        (tile,), name="last",
    )
    return (jnp.transpose(new_places, (1, 0, 2))[None], jnp.transpose(new_vortices, (1, 0, 2))[None])


def solution(mesh):
    in_specs = (
        P("stream", "cell", None, None),
        P("stream", "cell", None, None),
        P("stream", "cell"),
        P("stream", "cell", None, None),
        P("stream", "cell"),
        P("stream", "cell"),
        P("stream", "cell"),
    )
    out_specs = (P("stream", "cell", None, None), P("stream", "cell", None, None))
    return jax.shard_map(local, mesh=mesh, in_specs=in_specs, out_specs=out_specs, check_vma=False)
```

time: 161 us -> 155 us (0.963)
  the two profiles are of different devices: /device:TPU:24 before, /device:TPU:10 now
where the time goes in v2:
time: 155 us; the launch traced here: 154 us
  Pallas kernels  86.2 us (56%)
  starting transfers between devices  50.5 us (33%)
  local copies, waits for them, and re-layouts  7.96 us (5%)
  waiting for transfers between devices  7.38 us (5%)
    pallas_call x9, Pallas kernels, call(): pl.pallas_call(body, grid_spec=pltpu.PrefetchScalarGridSpec(num_scalar_pr...  86.2 us
    all_to_all x4, starting transfers between devices, exchange(): lax.all_to_all(value, 'cell', split_axis=0, concat_axis=0, tiled=True)  42.8 us
    unnamed x27, local copies, waits for them, and re-layouts  7.86 us
    ppermute x4, starting transfers between devices, shifted(): lax.ppermute(value, axis, [(source, source + steps) for source in range(l...  7.68 us
    ppermute x4, waiting for transfers between devices, shifted(): lax.ppermute(value, axis, [(source, source + steps) for source in range(l...  7.37 us
  transfers between devices with their start and end apart: 8, of which 2 were waited for; matrix products, arithmetic and copies ran while one was open for 0% of the time, Pallas kernels for 32%

profile of v2, /device:TPU:10, one launch (start us, length us, event | category | flops | bytes accessed | tf_op | source)
XLA Modules:
  0.0 154.3 jit_solution(2495966075472228777)
XLA Ops:
  0.6 0.8 copy.10
  1.4 0.1 reshape_squeeze.3.exports
  1.5 0.0 copy-start.3
  1.5 0.8 copy-done.3
  2.3 0.8 copy-done.5
  3.1 0.7 copy-done.11
  3.8 1.4 pack.1
  5.2 13.5 %all-to-all-start = ((f32[32,2,8,128]{3,2,1,0:T(8,128)}), f32[32,2,8,128]{3,2,1,0:T(8,128)S(1)}, u32[]{:S(2)}, u32[]{:S(2)}) async-start(f32[32,2,8,128]{3,2,1,0:T(8,128)} %bitcast.5), calls=%async_computation | async-start | bytes 524288 | tf_op jit(solution)/shard_map/all_to_all | solution.py:321
  18.7 1.9 %collective-permute-start = (f32[256,128]{1,0:T(8,128)S(1)}, f32[256,128]{1,0:T(8,128)S(1)}, u32[]{:S(2)}, u32[]{:S(2)}) collective-permute-start(f32[256,128]{1,0:T(8,128)S(1)} %get-tuple-element.25.cells_ref), channel_id=1, source_target_pairs={{0,32},{32,64},{64,96},{96,128},{128,160},{160,192},{192,224},{224... | collective-permute-start | bytes 393224 | tf_op jit(solution)/shard_map/ppermute | solution.py:28
  21.3 0.7 fusion
  22.0 3.0 %collective-permute-done.above_ref = f32[256,128]{1,0:T(8,128)S(1)} collective-permute-done((f32[256,128]{1,0:T(8,128)S(1)}, f32[256,128]{1,0:T(8,128)S(1)}, u32[]{:S(2)}, u32[]{:S(2)}) %collective-permute-start) | collective-permute-done | bytes 131104 | tf_op jit(solution)/shard_map/ppermute | solution.py:28
  25.0 9.6 %near.2 = (f32[256,128]{1,0:T(8,128)S(1)}, f32[256,128]{1,0:T(8,128)S(1)}, bf16[32,128,128]{2,1,0:T(8,128)(2,1)S(1)}, f32[32,3,128,128]{3,2,1,0:T(8,128)}) custom-call(f32[256,128]{1,0:T(8,128)S(1)} %get-tuple-element.25.cells_ref, f32[256,128]{1,0:T(8,128)S(1)} %collective-permute-done.above_ref), custom_call_target="tpu_custom_call" | custom-call | tf_op jit(solution)/shard_map/near/pallas_call | solution.py:290
  34.6 1.0 copy-done
  35.5 1.2 copy-done.1
  36.8 16.6 %far.2 = (f32[512,128]{1,0:T(8,128)}, bf16[64,128,128]{2,1,0:T(8,128)(2,1)S(1)}) custom-call(s32[192]{0:T(256)S(1)} %get-tuple-element.49.here_ids, s32[192]{0:T(256)S(1)} %get-tuple-element.48.there_ids, s32[1]{0:T(128)} %bitcast.28.count, f32[32,3,128,128]{3,2,1,0:T(8,128)} %get-tuple-element.29.cols_ref, bf16[32,128,128]{2,1,0:T(8,128)(2,1)S(1)} %copy-done.1, ...), custom_call_target="tpu_custom_call" | custom-call | tf_op jit(solution)/shard_map/far/pallas_call | solution.py:290
  53.4 9.8 %all-to-all-start.1 = ((f32[32,2,8,128]{3,2,1,0:T(8,128)}), f32[32,2,8,128]{3,2,1,0:T(8,128)S(1)}, u32[]{:S(2)}, u32[]{:S(2)}) async-start(f32[32,2,8,128]{3,2,1,0:T(8,128)} %bitcast.11), calls=%async_computation.1 | async-start | bytes 524288 | tf_op jit(solution)/shard_map/all_to_all | solution.py:321
  63.2 1.9 %collective-permute-start.1 = (f32[256,128]{1,0:T(8,128)S(1)}, f32[256,128]{1,0:T(8,128)S(1)}, u32[]{:S(2)}, u32[]{:S(2)}) collective-permute-start(f32[256,128]{1,0:T(8,128)S(1)} %get-tuple-element.33), channel_id=1, source_target_pairs={{32,0},{64,32},{96,64},{128,96},{160,128},{192,160},{224,192},{256... | collective-permute-start | bytes 393224 | tf_op jit(solution)/shard_map/ppermute | solution.py:28
  65.1 15.0 %here.2.remote = f32[256,128]{1,0:T(8,128)S(1)} custom-call(s32[192]{0:T(256)S(1)} %get-tuple-element.49.here_ids, s32[192]{0:T(256)S(1)} %get-tuple-element.48.there_ids, s32[1]{0:T(128)} %bitcast.29.count, f32[32,3,128,128]{3,2,1,0:T(8,128)} %get-tuple-element.29.cols_ref, bf16[64,128,128]{2,1,0:T(8,128)(2,1)S(1)} %get-tuple-element.32.wide_ref, ...), custom_call_target="tpu_custom_call" | custom-call | tf_op jit(solution)/shard_map/here/pallas_call | solution.py:290
  80.1 1.6 %middle.1 = (f32[256,128]{1,0:T(8,128)S(1)}, f32[256,128]{1,0:T(8,128)S(1)}, f32[512,128]{1,0:T(8,128)}) custom-call(s32[64]{0:T(128)S(1)} %reshape_squeeze.3.exports, f32[256,128]{1,0:T(8,128)S(1)} %get-tuple-element.25.cells_ref, f32[256,128]{1,0:T(8,128)S(1)} %get-tuple-element.28.near, f32[256,128]{1,0:T(8,128)S(1)} %here.2.remote, ...), custom_call_target="tpu_custom_call" | custom-call | tf_op jit(solution)/shard_map/middle/pallas_call | solution.py:290
  81.7 0.7 copy-done.7
  82.4 9.8 %all-to-all-start.2 = ((f32[32,2,8,128]{3,2,1,0:T(8,128)}), f32[32,2,8,128]{3,2,1,0:T(8,128)S(1)}, u32[]{:S(2)}, u32[]{:S(2)}) async-start(f32[32,2,8,128]{3,2,1,0:T(8,128)} %bitcast.13), calls=%async_computation.2 | async-start | bytes 524288 | tf_op jit(solution)/shard_map/all_to_all | solution.py:321
  92.2 1.9 %collective-permute-start.2 = (f32[256,128]{1,0:T(8,128)S(1)}, f32[256,128]{1,0:T(8,128)S(1)}, u32[]{:S(2)}, u32[]{:S(2)}) collective-permute-start(f32[256,128]{1,0:T(8,128)S(1)} %get-tuple-element.35.cells_ref), channel_id=1, source_target_pairs={{0,32},{32,64},{64,96},{96,128},{128,160},{160,192},{192,224},{224... | collective-permute-start | bytes 393224 | tf_op jit(solution)/shard_map/ppermute | solution.py:28
  94.1 4.4 %collective-permute-done.2.above_ref = f32[256,128]{1,0:T(8,128)S(1)} collective-permute-done((f32[256,128]{1,0:T(8,128)S(1)}, f32[256,128]{1,0:T(8,128)S(1)}, u32[]{:S(2)}, u32[]{:S(2)}) %collective-permute-start.2) | collective-permute-done | bytes 131104 | tf_op jit(solution)/shard_map/ppermute | solution.py:28
  98.5 9.6 %near.3 = (f32[256,128]{1,0:T(8,128)S(1)}, f32[256,128]{1,0:T(8,128)S(1)}, bf16[32,128,128]{2,1,0:T(8,128)(2,1)S(1)}, f32[32,3,128,128]{3,2,1,0:T(8,128)}) custom-call(f32[256,128]{1,0:T(8,128)S(1)} %get-tuple-element.35.cells_ref, f32[256,128]{1,0:T(8,128)S(1)} %collective-permute-done.2.above_ref), custom_call_target="tpu_custom_call" | custom-call | tf_op jit(solution)/shard_map/near/pallas_call | solution.py:290
  108.1 0.6 copy-done.9
  108.7 0.7 copy-done.12
  109.4 15.9 %far.3 = (f32[512,128]{1,0:T(8,128)S(1)}, bf16[64,128,128]{2,1,0:T(8,128)(2,1)S(1)}) custom-call(s32[192]{0:T(256)S(1)} %get-tuple-element.49.here_ids, s32[192]{0:T(256)S(1)} %get-tuple-element.48.there_ids, s32[1]{0:T(128)} %bitcast.30.count, f32[32,3,128,128]{3,2,1,0:T(8,128)} %get-tuple-element.39.cols_ref, ...), custom_call_target="tpu_custom_call" | custom-call | tf_op jit(solution)/shard_map/far/pallas_call | solution.py:290
  125.3 0.7 copy-done.2
  126.0 9.8 %all-to-all-start.3 = ((f32[32,2,8,128]{3,2,1,0:T(8,128)}), f32[32,2,8,128]{3,2,1,0:T(8,128)S(1)}, u32[]{:S(2)}, u32[]{:S(2)}) async-start(f32[32,2,8,128]{3,2,1,0:T(8,128)} %bitcast.38), calls=%async_computation.3 | async-start | bytes 524288 | tf_op jit(solution)/shard_map/all_to_all | solution.py:321
  135.8 1.9 %collective-permute-start.3 = (f32[256,128]{1,0:T(8,128)}, f32[256,128]{1,0:T(8,128)S(1)}, u32[]{:S(2)}, u32[]{:S(2)}) collective-permute-start(f32[256,128]{1,0:T(8,128)} %copy-done.12), channel_id=1, source_target_pairs={{32,0},{64,32},{96,64},{128,96},{160,128},{192,160},{224,192},{256... | collective-permute-start | bytes 393224 | tf_op jit(solution)/shard_map/ppermute | solution.py:28
  137.7 15.0 %here.3.remote = f32[256,128]{1,0:T(8,128)S(1)} custom-call(s32[192]{0:T(256)S(1)} %get-tuple-element.49.here_ids, s32[192]{0:T(256)S(1)} %get-tuple-element.48.there_ids, s32[1]{0:T(128)} %bitcast.31.count, f32[32,3,128,128]{3,2,1,0:T(8,128)} %get-tuple-element.39.cols_ref, bf16[64,128,128]{2,1,0:T(8,128)(2,1)S(1)} %get-tuple-element.42.wide_ref, ...), custom_call_target="tpu_custom_call" | custom-call | tf_op jit(solution)/shard_map/here/pallas_call | solution.py:290
  152.7 1.5 last.1
  (22 shorter events, 0.1 us)
Async XLA Ops:
  1.5 0.8 copy-start.3
  2.3 0.8 copy-start.5
  3.1 0.7 copy-start.11
  5.2 30.3 %all-to-all-start = ((f32[32,2,8,128]{3,2,1,0:T(8,128)}), f32[32,2,8,128]{3,2,1,0:T(8,128)S(1)}, u32[]{:S(2)}, u32[]{:S(2)}) async-start(f32[32,2,8,128]{3,2,1,0:T(8,128)} %bitcast.5), calls=%async_computation | async-start | bytes 524288 | tf_op jit(solution)/shard_map/all_to_all | solution.py:321
  18.7 6.3 %collective-permute-start = (f32[256,128]{1,0:T(8,128)S(1)}, f32[256,128]{1,0:T(8,128)S(1)}, u32[]{:S(2)}, u32[]{:S(2)}) collective-permute-start(f32[256,128]{1,0:T(8,128)S(1)} %get-tuple-element.25.cells_ref), channel_id=1, source_target_pairs={{0,32},{32,64},{64,96},{96,128},{128,160},{160,192},{192,224},{224... | collective-permute-start | bytes 393224 | tf_op jit(solution)/shard_map/ppermute | solution.py:28
  34.6 1.0 copy-start
  35.5 1.2 copy-start.1
  53.4 26.7 %all-to-all-start.1 = ((f32[32,2,8,128]{3,2,1,0:T(8,128)}), f32[32,2,8,128]{3,2,1,0:T(8,128)S(1)}, u32[]{:S(2)}, u32[]{:S(2)}) async-start(f32[32,2,8,128]{3,2,1,0:T(8,128)} %bitcast.11), calls=%async_computation.1 | async-start | bytes 524288 | tf_op jit(solution)/shard_map/all_to_all | solution.py:321
  63.2 16.9 %collective-permute-start.1 = (f32[256,128]{1,0:T(8,128)S(1)}, f32[256,128]{1,0:T(8,128)S(1)}, u32[]{:S(2)}, u32[]{:S(2)}) collective-permute-start(f32[256,128]{1,0:T(8,128)S(1)} %get-tuple-element.33), channel_id=1, source_target_pairs={{32,0},{64,32},{96,64},{128,96},{160,128},{192,160},{224,192},{256... | collective-permute-start | bytes 393224 | tf_op jit(solution)/shard_map/ppermute | solution.py:28
  81.7 0.7 copy-start.7
  82.4 27.0 %all-to-all-start.2 = ((f32[32,2,8,128]{3,2,1,0:T(8,128)}), f32[32,2,8,128]{3,2,1,0:T(8,128)S(1)}, u32[]{:S(2)}, u32[]{:S(2)}) async-start(f32[32,2,8,128]{3,2,1,0:T(8,128)} %bitcast.13), calls=%async_computation.2 | async-start | bytes 524288 | tf_op jit(solution)/shard_map/all_to_all | solution.py:321
  92.2 6.3 %collective-permute-start.2 = (f32[256,128]{1,0:T(8,128)S(1)}, f32[256,128]{1,0:T(8,128)S(1)}, u32[]{:S(2)}, u32[]{:S(2)}) collective-permute-start(f32[256,128]{1,0:T(8,128)S(1)} %get-tuple-element.35.cells_ref), channel_id=1, source_target_pairs={{0,32},{32,64},{64,96},{96,128},{128,160},{160,192},{192,224},{224... | collective-permute-start | bytes 393224 | tf_op jit(solution)/shard_map/ppermute | solution.py:28
  108.1 0.7 copy-start.9
  108.7 0.7 copy-start.12
  125.3 0.7 copy-start.2
  125.3 27.4 %copy-start.4 = (f32[1,32,3,128]{3,1,2,0:T(8,128)S(1)}, f32[1,32,3,128]{3,1,2,0:T(8,128)}, u32[]{:S(2)}) copy-start(f32[1,32,3,128]{3,1,2,0:T(8,128)} %param.7) | copy-start | bytes 147460
  125.3 27.4 %copy-start.6 = (f32[1,32,3,128]{3,1,2,0:T(8,128)S(1)}, f32[1,32,3,128]{3,1,2,0:T(8,128)}, u32[]{:S(2)}) copy-start(f32[1,32,3,128]{3,1,2,0:T(8,128)} %param.8) | copy-start | bytes 147460
  125.3 27.4 %copy-start.8 = (f32[256,128]{1,0:T(8,128)S(1)}, f32[256,128]{1,0:T(8,128)}, u32[]{:S(2)}) copy-start(f32[256,128]{1,0:T(8,128)} %copy-done.7) | copy-start | bytes 393220
  125.3 27.4 %copy-start.10 = (f32[256,128]{1,0:T(8,128)S(1)}, f32[256,128]{1,0:T(8,128)}, u32[]{:S(2)}) copy-start(f32[256,128]{1,0:T(8,128)} %copy-done.9) | copy-start | bytes 393220
  126.0 26.7 %all-to-all-start.3 = ((f32[32,2,8,128]{3,2,1,0:T(8,128)}), f32[32,2,8,128]{3,2,1,0:T(8,128)S(1)}, u32[]{:S(2)}, u32[]{:S(2)}) async-start(f32[32,2,8,128]{3,2,1,0:T(8,128)} %bitcast.38), calls=%async_computation.3 | async-start | bytes 524288 | tf_op jit(solution)/shard_map/all_to_all | solution.py:321
  135.8 16.9 %collective-permute-start.3 = (f32[256,128]{1,0:T(8,128)}, f32[256,128]{1,0:T(8,128)S(1)}, u32[]{:S(2)}, u32[]{:S(2)}) collective-permute-start(f32[256,128]{1,0:T(8,128)} %copy-done.12), channel_id=1, source_target_pairs={{32,0},{64,32},{96,64},{128,96},{160,128},{192,160},{224,192},{256... | collective-permute-start | bytes 393224 | tf_op jit(solution)/shard_map/ppermute | solution.py:28

commit v3 on v2

--- a/solution.py
+++ b/solution.py
@@ -18,6 +18,7 @@
 f32 = jnp.float32
 bf16 = jnp.bfloat16
 MOMENTS = 48
+UNROLL = 16
 NN = (((1,), (0,)), ((), ()))
 NT = (((1,), (1,)), ((), ()))
 
@@ -68,7 +69,7 @@
 def features(tile, base):
     x = [tile[k : k + 1] for k in range(3)]
     parts = []
-    for scale in (None, x[0], x[1], x[2], dot_rows(x, x)):
+    for scale in (None, x[0], x[1], x[2]):
         value = base if scale is None else scale * base
         high = value.astype(bf16).astype(f32)
         rest = value - high
@@ -76,7 +77,7 @@
         parts += [high, middle, rest - middle]
         if scale is None:
             parts.append(jnp.zeros((8, 128), f32))
-    return jnp.concatenate(parts, axis=0).astype(bf16)
+    return jnp.concatenate(parts + [jnp.zeros((8, 128), f32)], axis=0).astype(bf16)
 
 
 def columns(tile):
@@ -84,25 +85,28 @@
     return [jnp.broadcast_to(flipped[:, k : k + 1], (128, 128)) for k in range(3)]
 
 
-def weights(cols, tile):
+def weights(cols, tile, skip=None):
     d = [cols[k] - tile[k : k + 1] for k in range(3)]
     soft = dot_rows(d, d) + sigma_sq
     inverse = lax.rsqrt(soft)
     square = inverse * inverse
-    quintic = square * square * inverse
+    cubic = square * inverse
+    quintic = square * cubic
     smooth = jnp.exp2(soft * smooth_rate)
-    return split2(quintic), split2(smooth)
+    if skip is not None:
+        quintic, cubic, smooth = [jnp.where(skip, 0.0, value) for value in (quintic, cubic, smooth)]
+    return split2(quintic), split2(cubic), (smooth.astype(bf16),)
 
 
 def moments(wide, mats, dims):
-    side = 1 if dims is NT else 0
     twice = jnp.concatenate([wide, wide], axis=1)
-    quintic, smooth = [jnp.concatenate(parts, axis=side) for parts in mats]
-    q = lax.dot_general(twice, quintic, dims, preferred_element_type=f32)
-    s = lax.dot_general(twice[0:32], smooth, dims, preferred_element_type=f32)
-    starts = (0, 32, 56, 80, 104)
-    tiles = [q[k : k + 8] + q[k + 8 : k + 16] + q[k + 16 : k + 24] for k in starts]
-    return tiles + [s[0:8] + s[8:16] + s[16:24]]
+    out = []
+    for parts, left in zip(mats, (twice, twice[0:32], wide[0:32])):
+        right = jnp.concatenate(parts, axis=1 if dims is NT else 0) if len(parts) > 1 else parts[0]
+        sums = lax.dot_general(left, right, dims, preferred_element_type=f32)
+        starts = (0, 32, 56, 80) if left.shape[0] > 32 else (0,)
+        out += [sums[k : k + 8] + sums[k + 8 : k + 16] + sums[k + 16 : k + 24] for k in starts]
+    return out
 
 
 def put(target, c, tiles, add=False):
@@ -121,17 +125,12 @@
             return [moment[pl.ds(at + k, 8, stride=MOMENTS), :] for k in range(count)]
 
         x, a = cell_rows(0), cell_rows(3)
-        spin, norm = dot_rows(a, x), dot_rows(x, x) + sigma_sq
-        twice = [2.0 * x[k] for k in range(3)]
+        spin = dot_rows(a, x)
         parts = [sums(which, 0, 6) for which in range(5)]
         mixed = [
             spin * parts[0][r] - a[0] * parts[1][r] - a[1] * parts[2][r] - a[2] * parts[3][r] for r in range(6)
         ]
-        cubic = [
-            norm * parts[0][r] + parts[4][r]
-            - twice[0] * parts[1][r] - twice[1] * parts[2][r] - twice[2] * parts[3][r]
-            for r in range(6)
-        ]
+        cubic = parts[4]
         turn, drift = cross_rows(x, mixed[3:6]), cross_rows(x, cubic[3:6])
         twist = cross_rows(a, cubic[3:6])
         spread, total = sums(5, 3), sums(5, 6, 1)[0]
@@ -168,10 +167,13 @@
 
 
 def near_kernel(
-    cells_ref, above_ref, near_ref, far_ref, wide_ref, cols_out, base_here, base_there, mom_near, mom_far, kept, sem
+    cells_ref, above_ref, near_ref, far_ref, wide_out, cols_out,
+    base_here, base_there, mom_near, mom_far, wide_here, cols_here, sems,
 ):
     fill_bases(cells_ref, base_here)
     fill_bases(above_ref, base_there)
+    row, column = [lax.broadcasted_iota(jnp.int32, (128, 128), axis) for axis in (0, 1)]
+    itself = row == column
 
     def cell(c):
         here, there = tile_rows(cells_ref, c), tile_rows(above_ref, c)
@@ -181,25 +183,38 @@
         joint = weights(cols, there)
         near = moments(wide_there, joint, NT)
         far = moments(wide, joint, NN)
-        own = moments(wide, weights(cols, here), NN)
-        wide_ref[c] = wide
+        own = moments(wide, weights(cols, here, itself), NN)
+        wide_here[c, 0] = wide
         for k in range(3):
-            kept[c, k] = cols[k]
+            cols_here[c, k] = cols[k]
         put(mom_far, c, far)
         put(mom_near, c, [p + q for p, q in zip(near, own)])
 
-    unrolled(wide_ref.shape[0], 4, cell)
-    copy = pltpu.make_async_copy(kept, cols_out, sem)
-    copy.start()
+    half = wide_here.shape[0] // 2
+    copies = []
+    for part in range(2):
+        unrolled(half, 4, lambda c: cell(c + part * half))
+        rows = pl.ds(part * half, half)
+        for k, (kept, out) in enumerate(((wide_here, wide_out), (cols_here, cols_out))):
+            copies.append(pltpu.make_async_copy(kept.at[rows], out.at[rows], sems.at[part, k]))
+            copies[-1].start()
     credits(above_ref, mom_far, far_ref)
     credits(cells_ref, mom_near, near_ref)
-    copy.wait()
-
-
-def far_kernel(here_ids, there_ids, count, cols_ref, wide_ref, got_ref, far_ref, wide_out, cols, sem, base, mom):
+    for copy in copies:
+        copy.wait()
+
+
+def far_kernel(
+    here_ids, there_ids, count, wide_ref, cols_ref, got_ref, far_ref, wide_out,
+    wide_here, cols, sems, base, mom,
+):
     cells, imports = cols.shape[0], wide_out.shape[0]
-    copy = pltpu.make_async_copy(cols_ref, cols, sem)
-    copy.start()
+    copies = [
+        pltpu.make_async_copy(source, kept, sems.at[0, k])
+        for k, (source, kept) in enumerate(((wide_ref, wide_here), (cols_ref, cols)))
+    ]
+    for copy in copies:
+        copy.start()
     fill_bases(got_ref, base)
     mom[...] = jnp.zeros(mom.shape, f32)
 
@@ -207,20 +222,21 @@
         wide_out[b] = features(tile_rows(got_ref, b), tile_rows(base, b))
 
     unrolled(imports, 8, prepare)
-    copy.wait()
+    for copy in copies:
+        copy.wait()
 
     def pair(n):
         c, b = jnp.minimum(here_ids[n], cells - 1), there_ids[n]
         mats = weights([cols[c, k] for k in range(3)], tile_rows(got_ref, jnp.minimum(b, imports - 1)))
-        put(mom, b, moments(wide_ref[c], mats, NN), add=True)
+        put(mom, b, moments(wide_here[c, 0], mats, NN), add=True)
 
     pairs(count, pair)
     credits(got_ref, mom, far_ref)
 
 
-def here_kernel(here_ids, there_ids, count, cols_ref, wide_ref, got_ref, cells_ref, own_ref, cols, sem, mom):
+def here_kernel(here_ids, there_ids, count, cols_ref, wide_ref, got_ref, cells_ref, own_ref, cols, sems, mom):
     cells, imports = cols.shape[0], wide_ref.shape[0]
-    copy = pltpu.make_async_copy(cols_ref, cols, sem)
+    copy = pltpu.make_async_copy(cols_ref, cols, sems.at[0, 0])
     copy.start()
     mom[...] = jnp.zeros(mom.shape, f32)
     copy.wait()
@@ -237,11 +253,11 @@
 
 def pairs(count, pair):
     def trip(t, carry):
-        for u in range(16):
-            pair(t * 16 + u)
+        for u in range(UNROLL):
+            pair(t * UNROLL + u)
         return carry
 
-    lax.fori_loop(0, (count[0] + 15) // 16, trip, 0)
+    lax.fori_loop(0, (count[0] + UNROLL - 1) // UNROLL, trip, 0)
 
 
 def gather_rates(exports, cells_ref, parts, back_ref, total_ref):
@@ -277,27 +293,27 @@
 
 
 def call(body, scalars, arrays, outs, scratch=(), name=None):
-    def spec(shape):
-        return pl.BlockSpec(memory_space=pltpu.HBM if len(shape) == 4 else pltpu.VMEM)
-
-    def shape(out):
-        if len(out) == 4:
-            return pltpu.HBM(out, f32)
-        return jax.ShapeDtypeStruct(out, bf16 if len(out) == 3 and out[1] == 128 else f32)
-
-    outs = [shape(out) for out in outs]
+    def spec(one):
+        if len(one.shape) == 4:
+            return pl.BlockSpec(memory_space=pltpu.HBM)
+        zeros = (0,) * len(one.shape)
+        return pl.BlockSpec(one.shape, lambda i, *_: zeros, pipeline_mode=pl.Buffered(1))
+
+    outs = [out if len(out) == 2 and isinstance(out[0], tuple) else (out, f32) for out in outs]
+    outs = [pltpu.HBM(*out) if len(out[0]) == 4 else jax.ShapeDtypeStruct(*out) for out in outs]
     arrays = [pltpu.with_memory_space_constraint(one, pltpu.HBM) if one.ndim == 4 else one for one in arrays]
     return pl.pallas_call(
         body,
         grid_spec=pltpu.PrefetchScalarGridSpec(
             num_scalar_prefetch=len(scalars),
-            grid=(),
-            in_specs=[spec(array.shape) for array in arrays],
-            out_specs=[spec(out.shape) for out in outs],
+            grid=(1,),
+            in_specs=[spec(array) for array in arrays],
+            out_specs=[spec(out) for out in outs],
             scratch_shapes=[pltpu.VMEM(one, f32) if isinstance(one, tuple) else one for one in scratch],
         ),
         out_shape=outs,
         compiler_params=pltpu.CompilerParams(vmem_limit_bytes=20 << 20),
+        cost_estimate=pl.CostEstimate(flops=10**10 if name in ("near", "far", "here") else 10**8, bytes_accessed=10**6, transcendentals=0),
         name=name,
     )(*scalars, *arrays)
 
@@ -314,7 +330,8 @@
     here_ids = jnp.where(alive, pair_local[0], cells)
     there_ids = jnp.where(alive, pair_remote[0], imports)
     tile, traded = (cells * 8, 128), (imports * 8, 128)
-    spread, done = (cells, 3, 128, 128), pltpu.SemaphoreType.DMA
+    spread, gathered = (cells, 3, 128, 128), ((cells + 1) * MOMENTS, 128)
+    kept, sems = pltpu.VMEM((cells, 1, 112, 128), bf16), pltpu.SemaphoreType.DMA((2, 2))
 
     def exchange(value):
         value = value.reshape(owners, per_owner, 8, 128)
@@ -325,21 +342,20 @@
         above = shifted(packed, "stream", 1)
         got = exchange(sent)
         near, far, wide, cols = call(
-            near_kernel, (), (packed, above),
-            (tile, tile, (cells, 128, 128), spread),
-            (tile, tile, (cells * MOMENTS, 128), (cells * MOMENTS, 128), spread, done), name="near",
+            near_kernel, (), (packed, above), (tile, tile, ((cells, 1, 112, 128), bf16), spread),
+            (tile, tile, (cells * MOMENTS, 128), (cells * MOMENTS, 128), kept, spread, sems), name="near",
         )
         below = shifted(far, "stream", -1)
         got, near = lax.optimization_barrier((got, near))
         listed = (here_ids, there_ids, count)
         back, wide_there = call(
-            far_kernel, listed, (cols, wide, got), (traded, (imports, 128, 128)),
-            (spread, done, traded, ((imports + 1) * MOMENTS, 128)), name="far",
+            far_kernel, listed, (wide, cols, got), (traded, ((imports, 112, 128), bf16)),
+            (kept, spread, sems, traded, ((imports + 1) * MOMENTS, 128)), name="far",
         )
         returned = exchange(back)
         (remote,) = call(
             here_kernel, listed, (cols, wide_there, got, packed), (tile,),
-            (spread, done, ((cells + 1) * MOMENTS, 128),), name="here",
+            (spread, sems, gathered), name="here",
         )
         return near, remote, below, returned
 

time: 155 us -> 155 us (level)
  the two profiles are of different devices: /device:TPU:10 before, /device:TPU:38 now
where the time goes in v3:
time: 155 us; the launch traced here: 154 us
  Pallas kernels  92.2 us (59%)
  starting transfers between devices  52.2 us (34%)
  waiting for transfers between devices  4.24 us (3%)
  local copies, waits for them, and re-layouts  3.12 us (2%)
    pallas_call x9, Pallas kernels, call(): pl.pallas_call(body, grid_spec=pltpu.PrefetchScalarGridSpec(num_scalar_pr...  92.2 us
    all_to_all x4, starting transfers between devices, exchange(): lax.all_to_all(value, 'cell', split_axis=0, concat_axis=0, tiled=True)  42.2 us
    ppermute x4, starting transfers between devices, shifted(): lax.ppermute(value, axis, [(source, source + steps) for source in range(l...  10 us
    ppermute x4, waiting for transfers between devices, shifted(): lax.ppermute(value, axis, [(source, source + steps) for source in range(l...  4.23 us
  transfers between devices with their start and end apart: 8, of which 1 were waited for; matrix products, arithmetic and copies ran while one was open for 0% of the time, Pallas kernels for 57%

profile of v3, /device:TPU:38, one launch (start us, length us, event | category | flops | bytes accessed | tf_op | source)
XLA Modules:
  0.0 153.9 jit_solution(3964193489213584581)
XLA Ops:
  0.6 0.8 copy.10
  1.4 0.1 reshape_squeeze.3.exports
  1.5 0.0 copy-start
  1.5 0.8 copy-done
  2.3 0.8 copy-done.2
  3.1 0.7 copy-done.4
  3.8 1.4 pack.1
  5.2 13.5 %all-to-all-start = ((f32[32,2,8,128]{3,2,1,0:T(8,128)}), f32[32,2,8,128]{3,2,1,0:T(8,128)S(1)}, u32[]{:S(2)}, u32[]{:S(2)}) async-start(f32[32,2,8,128]{3,2,1,0:T(8,128)} %bitcast.5), calls=%async_computation | async-start | bytes 524288 | tf_op jit(solution)/shard_map/all_to_all | solution.py:338
  18.6 1.9 %collective-permute-start = (f32[256,128]{1,0:T(8,128)S(1)}, f32[256,128]{1,0:T(8,128)S(1)}, u32[]{:S(2)}, u32[]{:S(2)}) collective-permute-start(f32[256,128]{1,0:T(8,128)S(1)} %get-tuple-element.25.cells_ref), channel_id=1, source_target_pairs={{0,32},{32,64},{64,96},{96,128},{128,160},{160,192},{192,224},{224... | collective-permute-start | bytes 393224 | tf_op jit(solution)/shard_map/ppermute | solution.py:29
  21.2 0.7 fusion
  21.9 4.2 %collective-permute-done.above_ref = f32[256,128]{1,0:T(8,128)S(1)} collective-permute-done((f32[256,128]{1,0:T(8,128)S(1)}, f32[256,128]{1,0:T(8,128)S(1)}, u32[]{:S(2)}, u32[]{:S(2)}) %collective-permute-start) | collective-permute-done | bytes 131104 | tf_op jit(solution)/shard_map/ppermute | solution.py:29
  26.1 9.3 %near.2 = (f32[256,128]{1,0:T(8,128)S(1)}, f32[256,128]{1,0:T(8,128)S(1)}, bf16[32,1,112,128]{3,2,1,0:T(8,128)(2,1)}, f32[32,3,128,128]{3,2,1,0:T(8,128)}) custom-call(f32[256,128]{1,0:T(8,128)S(1)} %get-tuple-element.25.cells_ref, f32[256,128]{1,0:T(8,128)S(1)} %collective-permute-done.above_ref), custom_call_target="tpu_custom_call" | custom-call | flops 10000000000 | bytes 1000000 | tf_op jit(solution)/shard_map/near/pallas_call | solution.py:305
  35.4 1.9 %collective-permute-start.1 = (f32[256,128]{1,0:T(8,128)S(1)}, f32[256,128]{1,0:T(8,128)S(1)}, u32[]{:S(2)}, u32[]{:S(2)}) collective-permute-start(f32[256,128]{1,0:T(8,128)S(1)} %get-tuple-element.33), channel_id=1, source_target_pairs={{32,0},{64,32},{96,64},{128,96},{160,128},{192,160},{224,192},{256... | collective-permute-start | bytes 393224 | tf_op jit(solution)/shard_map/ppermute | solution.py:29
  37.3 0.0 all-to-all-done
  37.3 17.9 %far.2 = (f32[512,128]{1,0:T(8,128)}, bf16[64,112,128]{2,1,0:T(8,128)(2,1)S(1)}) custom-call(s32[192]{0:T(256)S(1)} %get-tuple-element.49.here_ids, s32[192]{0:T(256)S(1)} %get-tuple-element.48.there_ids, s32[1]{0:T(128)} %bitcast.28.count, bf16[32,1,112,128]{3,2,1,0:T(8,128)(2,1)} %get-tuple-element.30.wide_ref, ...), custom_call_target="tpu_custom_call" | custom-call | flops 10000000000 | bytes 1000000 | tf_op jit(solution)/shard_map/far/pallas_call | solution.py:305
  55.2 9.6 %all-to-all-start.1 = ((f32[32,2,8,128]{3,2,1,0:T(8,128)}), f32[32,2,8,128]{3,2,1,0:T(8,128)S(1)}, u32[]{:S(2)}, u32[]{:S(2)}) async-start(f32[32,2,8,128]{3,2,1,0:T(8,128)} %bitcast.11), calls=%async_computation.1 | async-start | bytes 524288 | tf_op jit(solution)/shard_map/all_to_all | solution.py:338
  64.8 16.7 %here.2.remote = f32[256,128]{1,0:T(8,128)S(1)} custom-call(s32[192]{0:T(256)S(1)} %get-tuple-element.49.here_ids, s32[192]{0:T(256)S(1)} %get-tuple-element.48.there_ids, s32[1]{0:T(128)} %bitcast.29.count, f32[32,3,128,128]{3,2,1,0:T(8,128)} %get-tuple-element.29.cols_ref, bf16[64,112,128]{2,1,0:T(8,128)(2,1)S(1)} %get-tuple-element.32.wide_ref, ...), custom_call_target="tpu_custom_call" | custom-call | flops 10000000000 | bytes 1000000 | tf_op jit(solution)/shard_map/here/pallas_call | solution.py:305
  81.5 0.0 collective-permute-done.1.below
  81.5 1.6 %middle.1 = (f32[256,128]{1,0:T(8,128)S(1)}, f32[256,128]{1,0:T(8,128)S(1)}, f32[512,128]{1,0:T(8,128)}) custom-call(s32[64]{0:T(128)S(1)} %reshape_squeeze.3.exports, f32[256,128]{1,0:T(8,128)S(1)} %get-tuple-element.25.cells_ref, f32[256,128]{1,0:T(8,128)S(1)} %get-tuple-element.28.near, f32[256,128]{1,0:T(8,128)S(1)} %here.2.remote, ...), custom_call_target="tpu_custom_call" | custom-call | flops 100000000 | bytes 1000000 | tf_op jit(solution)/shard_map/middle/pallas_call | solution.py:305
  83.1 1.9 %collective-permute-start.2 = (f32[256,128]{1,0:T(8,128)S(1)}, f32[256,128]{1,0:T(8,128)S(1)}, u32[]{:S(2)}, u32[]{:S(2)}) collective-permute-start(f32[256,128]{1,0:T(8,128)S(1)} %get-tuple-element.35.cells_ref), channel_id=1, source_target_pairs={{0,32},{32,64},{64,96},{96,128},{128,160},{160,192},{192,224},{224... | collective-permute-start | bytes 393224 | tf_op jit(solution)/shard_map/ppermute | solution.py:29
  85.0 9.5 %all-to-all-start.2 = ((f32[32,2,8,128]{3,2,1,0:T(8,128)}), f32[32,2,8,128]{3,2,1,0:T(8,128)S(1)}, u32[]{:S(2)}, u32[]{:S(2)}) async-start(f32[32,2,8,128]{3,2,1,0:T(8,128)} %bitcast.13), calls=%async_computation.2 | async-start | bytes 524288 | tf_op jit(solution)/shard_map/all_to_all | solution.py:338
  94.6 0.0 collective-permute-done.2.above_ref
  94.6 9.3 %near.3 = (f32[256,128]{1,0:T(8,128)S(1)}, f32[256,128]{1,0:T(8,128)S(1)}, bf16[32,1,112,128]{3,2,1,0:T(8,128)(2,1)}, f32[32,3,128,128]{3,2,1,0:T(8,128)}) custom-call(f32[256,128]{1,0:T(8,128)S(1)} %get-tuple-element.35.cells_ref, f32[256,128]{1,0:T(8,128)S(1)} %collective-permute-done.2.above_ref), custom_call_target="tpu_custom_call" | custom-call | flops 10000000000 | bytes 1000000 | tf_op jit(solution)/shard_map/near/pallas_call | solution.py:305
  103.9 4.3 %collective-permute-start.3 = (f32[256,128]{1,0:T(8,128)S(1)}, f32[256,128]{1,0:T(8,128)S(1)}, u32[]{:S(2)}, u32[]{:S(2)}) collective-permute-start(f32[256,128]{1,0:T(8,128)S(1)} %get-tuple-element.43), channel_id=1, source_target_pairs={{32,0},{64,32},{96,64},{128,96},{160,128},{192,160},{224,192},{256... | collective-permute-start | bytes 393224 | tf_op jit(solution)/shard_map/ppermute | solution.py:29
  108.2 0.0 all-to-all-done.2
  108.2 17.9 %far.3 = (f32[512,128]{1,0:T(8,128)}, bf16[64,112,128]{2,1,0:T(8,128)(2,1)S(1)}) custom-call(s32[192]{0:T(256)S(1)} %get-tuple-element.49.here_ids, s32[192]{0:T(256)S(1)} %get-tuple-element.48.there_ids, s32[1]{0:T(128)} %bitcast.30.count, bf16[32,1,112,128]{3,2,1,0:T(8,128)(2,1)} %get-tuple-element.40.wide_ref, ...), custom_call_target="tpu_custom_call" | custom-call | flops 10000000000 | bytes 1000000 | tf_op jit(solution)/shard_map/far/pallas_call | solution.py:305
  126.0 9.6 %all-to-all-start.3 = ((f32[32,2,8,128]{3,2,1,0:T(8,128)}), f32[32,2,8,128]{3,2,1,0:T(8,128)S(1)}, u32[]{:S(2)}, u32[]{:S(2)}) async-start(f32[32,2,8,128]{3,2,1,0:T(8,128)} %bitcast.15), calls=%async_computation.3 | async-start | bytes 524288 | tf_op jit(solution)/shard_map/all_to_all | solution.py:338
  135.6 0.0 copy-start.1
  135.7 0.0 copy-start.3
  135.7 16.7 %here.3.remote = f32[256,128]{1,0:T(8,128)S(1)} custom-call(s32[192]{0:T(256)S(1)} %get-tuple-element.49.here_ids, s32[192]{0:T(256)S(1)} %get-tuple-element.48.there_ids, s32[1]{0:T(128)} %bitcast.31.count, f32[32,3,128,128]{3,2,1,0:T(8,128)} %get-tuple-element.39.cols_ref, bf16[64,112,128]{2,1,0:T(8,128)(2,1)S(1)} %get-tuple-element.42.wide_ref, ...), custom_call_target="tpu_custom_call" | custom-call | flops 10000000000 | bytes 1000000 | tf_op jit(solution)/shard_map/here/pallas_call | solution.py:305
  152.4 0.0 collective-permute-done.3.below
  152.4 1.5 last.1
  (6 shorter events, 0.0 us)
Async XLA Ops:
  1.5 0.8 copy-start
  2.3 0.8 copy-start.2
  3.1 0.7 copy-start.4
  5.2 32.2 %all-to-all-start = ((f32[32,2,8,128]{3,2,1,0:T(8,128)}), f32[32,2,8,128]{3,2,1,0:T(8,128)S(1)}, u32[]{:S(2)}, u32[]{:S(2)}) async-start(f32[32,2,8,128]{3,2,1,0:T(8,128)} %bitcast.5), calls=%async_computation | async-start | bytes 524288 | tf_op jit(solution)/shard_map/all_to_all | solution.py:338
  18.6 7.5 %collective-permute-start = (f32[256,128]{1,0:T(8,128)S(1)}, f32[256,128]{1,0:T(8,128)S(1)}, u32[]{:S(2)}, u32[]{:S(2)}) collective-permute-start(f32[256,128]{1,0:T(8,128)S(1)} %get-tuple-element.25.cells_ref), channel_id=1, source_target_pairs={{0,32},{32,64},{64,96},{96,128},{128,160},{160,192},{192,224},{224... | collective-permute-start | bytes 393224 | tf_op jit(solution)/shard_map/ppermute | solution.py:29
  35.4 46.1 %collective-permute-start.1 = (f32[256,128]{1,0:T(8,128)S(1)}, f32[256,128]{1,0:T(8,128)S(1)}, u32[]{:S(2)}, u32[]{:S(2)}) collective-permute-start(f32[256,128]{1,0:T(8,128)S(1)} %get-tuple-element.33), channel_id=1, source_target_pairs={{32,0},{64,32},{96,64},{128,96},{160,128},{192,160},{224,192},{256... | collective-permute-start | bytes 393224 | tf_op jit(solution)/shard_map/ppermute | solution.py:29
  55.2 26.3 %all-to-all-start.1 = ((f32[32,2,8,128]{3,2,1,0:T(8,128)}), f32[32,2,8,128]{3,2,1,0:T(8,128)S(1)}, u32[]{:S(2)}, u32[]{:S(2)}) async-start(f32[32,2,8,128]{3,2,1,0:T(8,128)} %bitcast.11), calls=%async_computation.1 | async-start | bytes 524288 | tf_op jit(solution)/shard_map/all_to_all | solution.py:338
  83.1 11.5 %collective-permute-start.2 = (f32[256,128]{1,0:T(8,128)S(1)}, f32[256,128]{1,0:T(8,128)S(1)}, u32[]{:S(2)}, u32[]{:S(2)}) collective-permute-start(f32[256,128]{1,0:T(8,128)S(1)} %get-tuple-element.35.cells_ref), channel_id=1, source_target_pairs={{0,32},{32,64},{64,96},{96,128},{128,160},{160,192},{192,224},{224... | collective-permute-start | bytes 393224 | tf_op jit(solution)/shard_map/ppermute | solution.py:29
  85.0 23.1 %all-to-all-start.2 = ((f32[32,2,8,128]{3,2,1,0:T(8,128)}), f32[32,2,8,128]{3,2,1,0:T(8,128)S(1)}, u32[]{:S(2)}, u32[]{:S(2)}) async-start(f32[32,2,8,128]{3,2,1,0:T(8,128)} %bitcast.13), calls=%async_computation.2 | async-start | bytes 524288 | tf_op jit(solution)/shard_map/all_to_all | solution.py:338
  103.9 48.5 %collective-permute-start.3 = (f32[256,128]{1,0:T(8,128)S(1)}, f32[256,128]{1,0:T(8,128)S(1)}, u32[]{:S(2)}, u32[]{:S(2)}) collective-permute-start(f32[256,128]{1,0:T(8,128)S(1)} %get-tuple-element.43), channel_id=1, source_target_pairs={{32,0},{64,32},{96,64},{128,96},{160,128},{192,160},{224,192},{256... | collective-permute-start | bytes 393224 | tf_op jit(solution)/shard_map/ppermute | solution.py:29
  126.0 26.3 %all-to-all-start.3 = ((f32[32,2,8,128]{3,2,1,0:T(8,128)}), f32[32,2,8,128]{3,2,1,0:T(8,128)S(1)}, u32[]{:S(2)}, u32[]{:S(2)}) async-start(f32[32,2,8,128]{3,2,1,0:T(8,128)} %bitcast.15), calls=%async_computation.3 | async-start | bytes 524288 | tf_op jit(solution)/shard_map/all_to_all | solution.py:338
  135.6 16.7 %copy-start.1 = (f32[1,32,3,128]{3,1,2,0:T(8,128)S(1)}, f32[1,32,3,128]{3,1,2,0:T(8,128)}, u32[]{:S(2)}) copy-start(f32[1,32,3,128]{3,1,2,0:T(8,128)} %param.7) | copy-start | bytes 147460
  135.7 16.7 %copy-start.3 = (f32[1,32,3,128]{3,1,2,0:T(8,128)S(1)}, f32[1,32,3,128]{3,1,2,0:T(8,128)}, u32[]{:S(2)}) copy-start(f32[1,32,3,128]{3,1,2,0:T(8,128)} %param.8) | copy-start | bytes 147460

commit v4 on v3

--- a/solution.py
+++ b/solution.py
@@ -19,6 +19,7 @@
 bf16 = jnp.bfloat16
 MOMENTS = 48
 UNROLL = 16
+HIDDEN = 8
 NN = (((1,), (0,)), ((), ()))
 NT = (((1,), (1,)), ((), ()))
 
@@ -149,7 +150,15 @@
     return ref[pl.ds(pl.multiple_of(c * 8, 8), 8), :]
 
 
-def pack_kernel(fill, exports, places, vortices, cells_ref, sent_ref):
+def pack_kernel(fill, exports, places_ref, vortices_ref, cells_ref, sent_ref, places, vortices, sems):
+    copies = [
+        pltpu.make_async_copy(source.at[0], kept, sems.at[0, k])
+        for k, (source, kept) in enumerate(((places_ref, places), (vortices_ref, vortices)))
+    ]
+    for copy in copies:
+        copy.start()
+    for copy in copies:
+        copy.wait()
     lane = lax.broadcasted_iota(jnp.int32, (1, 128), 1)
     for c in range(cells_ref.shape[0] // 8):
         mask = (lane < fill[c]).astype(f32)
@@ -205,8 +214,8 @@
 
 
 def far_kernel(
-    here_ids, there_ids, count, wide_ref, cols_ref, got_ref, far_ref, wide_out,
-    wide_here, cols, sems, base, mom,
+    here_ids, there_ids, count, wide_ref, cols_ref, got_ref, far_ref, wide_out, begun_ref,
+    wide_here, cols, sems, base, mom, mom_here,
 ):
     cells, imports = cols.shape[0], wide_out.shape[0]
     copies = [
@@ -217,6 +226,7 @@
         copy.start()
     fill_bases(got_ref, base)
     mom[...] = jnp.zeros(mom.shape, f32)
+    mom_here[...] = jnp.zeros(mom_here.shape, f32)
 
     def prepare(b):
         wide_out[b] = features(tile_rows(got_ref, b), tile_rows(base, b))
@@ -225,21 +235,33 @@
     for copy in copies:
         copy.wait()
 
-    def pair(n):
-        c, b = jnp.minimum(here_ids[n], cells - 1), there_ids[n]
-        mats = weights([cols[c, k] for k in range(3)], tile_rows(got_ref, jnp.minimum(b, imports - 1)))
-        put(mom, b, moments(wide_here[c, 0], mats, NN), add=True)
-
-    pairs(count, pair)
+    def pair(n, both):
+        c, b = here_ids[n], there_ids[n]
+        cell, source = jnp.minimum(c, cells - 1), jnp.minimum(b, imports - 1)
+        mats = weights([cols[cell, k] for k in range(3)], tile_rows(got_ref, source))
+        put(mom, b, moments(wide_here[cell, 0], mats, NN), add=True)
+        if both:
+            put(mom_here, c, moments(wide_out[source], mats, NT), add=True)
+
+    joint, total = trips(count)
+    pairs(0, joint, lambda n: pair(n, True))
+    begun = pltpu.make_async_copy(mom_here, begun_ref, sems.at[1, 0])
+    begun.start()
+    pairs(joint, total, lambda n: pair(n, False))
     credits(got_ref, mom, far_ref)
-
-
-def here_kernel(here_ids, there_ids, count, cols_ref, wide_ref, got_ref, cells_ref, own_ref, cols, sems, mom):
+    begun.wait()
+
+
+def here_kernel(here_ids, there_ids, count, cols_ref, wide_ref, got_ref, cells_ref, begun_ref, own_ref, cols, sems, mom):
     cells, imports = cols.shape[0], wide_ref.shape[0]
-    copy = pltpu.make_async_copy(cols_ref, cols, sems.at[0, 0])
-    copy.start()
-    mom[...] = jnp.zeros(mom.shape, f32)
-    copy.wait()
+    copies = [
+        pltpu.make_async_copy(source, kept, sems.at[0, k])
+        for k, (source, kept) in enumerate(((cols_ref, cols), (begun_ref, mom)))
+    ]
+    for copy in copies:
+        copy.start()
+    for copy in copies:
+        copy.wait()
 
     def pair(n):
         c, b = here_ids[n], jnp.minimum(there_ids[n], imports - 1)
@@ -247,17 +269,22 @@
         mats = weights([cols[cell, k] for k in range(3)], tile_rows(got_ref, b))
         put(mom, c, moments(wide_ref[b], mats, NT), add=True)
 
-    pairs(count, pair)
+    pairs(*trips(count), pair)
     credits(cells_ref, mom, own_ref)
 
 
-def pairs(count, pair):
+def trips(count):
+    total = (count[0] + UNROLL - 1) // UNROLL
+    return jnp.maximum(total - HIDDEN, 0), total
+
+
+def pairs(first, last, pair):
     def trip(t, carry):
         for u in range(UNROLL):
             pair(t * UNROLL + u)
         return carry
 
-    lax.fori_loop(0, (count[0] + UNROLL - 1) // UNROLL, trip, 0)
+    lax.fori_loop(first, last, trip, 0)
 
 
 def gather_rates(exports, cells_ref, parts, back_ref, total_ref):
@@ -292,16 +319,19 @@
             new_vortices[k, c : c + 1] = vortices[k, c : c + 1] + change[3 + k : 4 + k]
 
 
-def call(body, scalars, arrays, outs, scratch=(), name=None):
+def call(body, scalars, arrays, outs, scratch=(), name=None, held=()):
+    def stays(shape):
+        return len(shape) == 4 or shape in held
+
     def spec(one):
-        if len(one.shape) == 4:
+        if stays(one.shape):
             return pl.BlockSpec(memory_space=pltpu.HBM)
         zeros = (0,) * len(one.shape)
         return pl.BlockSpec(one.shape, lambda i, *_: zeros, pipeline_mode=pl.Buffered(1))
 
     outs = [out if len(out) == 2 and isinstance(out[0], tuple) else (out, f32) for out in outs]
-    outs = [pltpu.HBM(*out) if len(out[0]) == 4 else jax.ShapeDtypeStruct(*out) for out in outs]
-    arrays = [pltpu.with_memory_space_constraint(one, pltpu.HBM) if one.ndim == 4 else one for one in arrays]
+    outs = [pltpu.HBM(*out) if stays(out[0]) else jax.ShapeDtypeStruct(*out) for out in outs]
+    arrays = [pltpu.with_memory_space_constraint(one, pltpu.HBM) if stays(one.shape) else one for one in arrays]
     return pl.pallas_call(
         body,
         grid_spec=pltpu.PrefetchScalarGridSpec(
@@ -348,18 +378,18 @@
         below = shifted(far, "stream", -1)
         got, near = lax.optimization_barrier((got, near))
         listed = (here_ids, there_ids, count)
-        back, wide_there = call(
-            far_kernel, listed, (wide, cols, got), (traded, ((imports, 112, 128), bf16)),
-            (kept, spread, sems, traded, ((imports + 1) * MOMENTS, 128)), name="far",
+        back, wide_there, begun = call(
+            far_kernel, listed, (wide, cols, got), (traded, ((imports, 112, 128), bf16), gathered),
+            (kept, spread, sems, traded, ((imports + 1) * MOMENTS, 128), gathered), name="far", held=(gathered,),
         )
         returned = exchange(back)
         (remote,) = call(
-            here_kernel, listed, (cols, wide_there, got, packed), (tile,),
-            (spread, sems, gathered), name="here",
+            here_kernel, listed, (cols, wide_there, got, packed, begun), (tile,),
+            (spread, sems, gathered), name="here", held=(gathered,),
         )
         return near, remote, below, returned
 
-    packed, sent = call(pack_kernel, (fill[0], exports), (places, vortices), (tile, traded), name="pack")
+    packed, sent = call(pack_kernel, (fill[0], exports), (places[None], vortices[None]), (tile, traded), (places.shape, places.shape, sems), name="pack")
     first, middle, sent = call(
         middle_kernel, (exports,), (packed, *rates(packed, sent)), (tile, tile, traded), name="middle"
     )

time: 155 us -> 148 us (0.955)
  the two profiles are of different devices: /device:TPU:38 before, /device:TPU:35 now
where the time goes in v4:
time: 148 us; the launch traced here: 147 us
  Pallas kernels  76 us (51%)
  starting transfers between devices  66.5 us (45%)
  local copies, waits for them, and re-layouts  1.53 us (1%)
  between operations  1.5 us (1%)
    pallas_call x9, Pallas kernels, call(): pl.pallas_call(body, grid_spec=pltpu.PrefetchScalarGridSpec(num_scalar_pr...  76 us
    all_to_all x4, starting transfers between devices, exchange(): lax.all_to_all(value, 'cell', split_axis=0, concat_axis=0, tiled=True)  52.9 us
    ppermute x4, starting transfers between devices, shifted(): lax.ppermute(value, axis, [(source, source + steps) for source in range(l...  13.6 us
  transfers between devices with their start and end apart: 8, of which 1 were waited for; matrix products, arithmetic and copies ran while one was open for 0% of the time, Pallas kernels for 48%

profile of v4, /device:TPU:35, one launch (start us, length us, event | category | flops | bytes accessed | tf_op | source)
XLA Modules:
  0.0 146.9 jit_solution(7728708916558596040)
XLA Ops:
  0.6 0.8 copy.10
  1.4 0.1 reshape_squeeze.3.exports
  1.5 0.0 copy-start.2
  1.5 0.6 copy-done.2
  2.2 2.3 %pack.1 = (f32[256,128]{1,0:T(8,128)S(1)}, f32[512,128]{1,0:T(8,128)}) custom-call(s32[32]{0:T(128)S(1)} %bitcast.46, s32[64]{0:T(128)S(1)} %reshape_squeeze.3.exports, f32[1,3,32,128]{3,2,1,0:T(8,128)} %bitcast.42, f32[1,3,32,128]{3,2,1,0:T(8,128)} %bitcast.44), custom_call_target="tpu_custom_call" | custom-call | flops 100000000 | bytes 1000000 | tf_op jit(solution)/shard_map/pack/pallas_call | solution.py:335
  4.5 12.9 %all-to-all-start = ((f32[32,2,8,128]{3,2,1,0:T(8,128)}), f32[32,2,8,128]{3,2,1,0:T(8,128)S(1)}, u32[]{:S(2)}, u32[]{:S(2)}) async-start(f32[32,2,8,128]{3,2,1,0:T(8,128)} %bitcast.7), calls=%async_computation | async-start | bytes 524288 | tf_op jit(solution)/shard_map/all_to_all | solution.py:368
  17.4 3.4 %collective-permute-start = (f32[256,128]{1,0:T(8,128)S(1)}, f32[256,128]{1,0:T(8,128)S(1)}, u32[]{:S(2)}, u32[]{:S(2)}) collective-permute-start(f32[256,128]{1,0:T(8,128)S(1)} %get-tuple-element.27.cells_ref), channel_id=1, source_target_pairs={{0,32},{32,64},{64,96},{96,128},{128,160},{160,192},{192,224},{224... | collective-permute-start | bytes 393224 | tf_op jit(solution)/shard_map/ppermute | solution.py:30
  21.5 0.7 fusion
  22.2 0.6 collective-permute-done.above_ref
  22.8 9.3 %near.2 = (f32[256,128]{1,0:T(8,128)S(1)}, f32[256,128]{1,0:T(8,128)S(1)}, bf16[32,1,112,128]{3,2,1,0:T(8,128)(2,1)}, f32[32,3,128,128]{3,2,1,0:T(8,128)}) custom-call(f32[256,128]{1,0:T(8,128)S(1)} %get-tuple-element.27.cells_ref, f32[256,128]{1,0:T(8,128)S(1)} %collective-permute-done.above_ref), custom_call_target="tpu_custom_call" | custom-call | flops 10000000000 | bytes 1000000 | tf_op jit(solution)/shard_map/near/pallas_call | solution.py:335
  32.0 5.3 %collective-permute-start.1 = (f32[256,128]{1,0:T(8,128)S(1)}, f32[256,128]{1,0:T(8,128)S(1)}, u32[]{:S(2)}, u32[]{:S(2)}) collective-permute-start(f32[256,128]{1,0:T(8,128)S(1)} %get-tuple-element.36), channel_id=1, source_target_pairs={{32,0},{64,32},{96,64},{128,96},{160,128},{192,160},{224,192},{256... | collective-permute-start | bytes 393224 | tf_op jit(solution)/shard_map/ppermute | solution.py:30
  37.3 0.0 all-to-all-done
  37.3 13.6 %far.2 = (f32[512,128]{1,0:T(8,128)}, bf16[64,112,128]{2,1,0:T(8,128)(2,1)S(1)}, f32[1584,128]{1,0:T(8,128)}) custom-call(s32[192]{0:T(256)S(1)} %get-tuple-element.53.here_ids, s32[192]{0:T(256)S(1)} %get-tuple-element.52.there_ids, s32[1]{0:T(128)} %bitcast.32.count, bf16[32,1,112,128]{3,2,1,0:T(8,128)(2,1)} %get-tuple-element.32.wide_ref, ...), custom_call_target="tpu_custom_call" | custom-call | flops 10000000000 | bytes 1000000 | tf_op jit(solution)/shard_map/far/pallas_call | solution.py:335
  50.9 15.4 %all-to-all-start.1 = ((f32[32,2,8,128]{3,2,1,0:T(8,128)}), f32[32,2,8,128]{3,2,1,0:T(8,128)S(1)}, u32[]{:S(2)}, u32[]{:S(2)}) async-start(f32[32,2,8,128]{3,2,1,0:T(8,128)} %bitcast.13), calls=%async_computation.1 | async-start | bytes 524288 | tf_op jit(solution)/shard_map/all_to_all | solution.py:368
  66.3 12.5 %here.2.remote = f32[256,128]{1,0:T(8,128)S(1)} custom-call(s32[192]{0:T(256)S(1)} %get-tuple-element.53.here_ids, s32[192]{0:T(256)S(1)} %get-tuple-element.52.there_ids, s32[1]{0:T(128)} %bitcast.33.count, f32[32,3,128,128]{3,2,1,0:T(8,128)} %get-tuple-element.31.cols_ref, bf16[64,112,128]{2,1,0:T(8,128)(2,1)S(1)} %get-tuple-element.34.wide_ref, ...), custom_call_target="tpu_custom_call" | custom-call | flops 10000000000 | bytes 1000000 | tf_op jit(solution)/shard_map/here/pallas_call | solution.py:335
  78.8 0.0 collective-permute-done.1.below
  78.8 0.0 all-to-all-done.1
  78.8 1.6 %middle.1 = (f32[256,128]{1,0:T(8,128)S(1)}, f32[256,128]{1,0:T(8,128)S(1)}, f32[512,128]{1,0:T(8,128)}) custom-call(s32[64]{0:T(128)S(1)} %reshape_squeeze.3.exports, f32[256,128]{1,0:T(8,128)S(1)} %get-tuple-element.27.cells_ref, f32[256,128]{1,0:T(8,128)S(1)} %get-tuple-element.30.near, f32[256,128]{1,0:T(8,128)S(1)} %here.2.remote, ...), custom_call_target="tpu_custom_call" | custom-call | flops 100000000 | bytes 1000000 | tf_op jit(solution)/shard_map/middle/pallas_call | solution.py:335
  80.4 1.9 %collective-permute-start.2 = (f32[256,128]{1,0:T(8,128)S(1)}, f32[256,128]{1,0:T(8,128)S(1)}, u32[]{:S(2)}, u32[]{:S(2)}) collective-permute-start(f32[256,128]{1,0:T(8,128)S(1)} %get-tuple-element.38.cells_ref), channel_id=1, source_target_pairs={{0,32},{32,64},{64,96},{96,128},{128,160},{160,192},{192,224},{224... | collective-permute-start | bytes 393224 | tf_op jit(solution)/shard_map/ppermute | solution.py:30
  82.3 9.0 %all-to-all-start.2 = ((f32[32,2,8,128]{3,2,1,0:T(8,128)}), f32[32,2,8,128]{3,2,1,0:T(8,128)S(1)}, u32[]{:S(2)}, u32[]{:S(2)}) async-start(f32[32,2,8,128]{3,2,1,0:T(8,128)} %bitcast.15), calls=%async_computation.2 | async-start | bytes 524288 | tf_op jit(solution)/shard_map/all_to_all | solution.py:368
  91.4 0.0 collective-permute-done.2.above_ref
  91.4 9.3 %near.3 = (f32[256,128]{1,0:T(8,128)S(1)}, f32[256,128]{1,0:T(8,128)S(1)}, bf16[32,1,112,128]{3,2,1,0:T(8,128)(2,1)}, f32[32,3,128,128]{3,2,1,0:T(8,128)}) custom-call(f32[256,128]{1,0:T(8,128)S(1)} %get-tuple-element.38.cells_ref, f32[256,128]{1,0:T(8,128)S(1)} %collective-permute-done.2.above_ref), custom_call_target="tpu_custom_call" | custom-call | flops 10000000000 | bytes 1000000 | tf_op jit(solution)/shard_map/near/pallas_call | solution.py:335
  100.6 3.0 %collective-permute-start.3 = (f32[256,128]{1,0:T(8,128)S(1)}, f32[256,128]{1,0:T(8,128)S(1)}, u32[]{:S(2)}, u32[]{:S(2)}) collective-permute-start(f32[256,128]{1,0:T(8,128)S(1)} %get-tuple-element.47), channel_id=1, source_target_pairs={{32,0},{64,32},{96,64},{128,96},{160,128},{192,160},{224,192},{256... | collective-permute-start | bytes 393224 | tf_op jit(solution)/shard_map/ppermute | solution.py:30
  103.6 0.0 all-to-all-done.2
  103.6 13.6 %far.3 = (f32[512,128]{1,0:T(8,128)}, bf16[64,112,128]{2,1,0:T(8,128)(2,1)S(1)}, f32[1584,128]{1,0:T(8,128)}) custom-call(s32[192]{0:T(256)S(1)} %get-tuple-element.53.here_ids, s32[192]{0:T(256)S(1)} %get-tuple-element.52.there_ids, s32[1]{0:T(128)} %bitcast.34.count, bf16[32,1,112,128]{3,2,1,0:T(8,128)(2,1)} %get-tuple-element.43.wide_ref, ...), custom_call_target="tpu_custom_call" | custom-call | flops 10000000000 | bytes 1000000 | tf_op jit(solution)/shard_map/far/pallas_call | solution.py:335
  117.2 15.6 %all-to-all-start.3 = ((f32[32,2,8,128]{3,2,1,0:T(8,128)}), f32[32,2,8,128]{3,2,1,0:T(8,128)S(1)}, u32[]{:S(2)}, u32[]{:S(2)}) async-start(f32[32,2,8,128]{3,2,1,0:T(8,128)} %bitcast.17), calls=%async_computation.3 | async-start | bytes 524288 | tf_op jit(solution)/shard_map/all_to_all | solution.py:368
  132.8 0.0 copy-start
  132.8 0.0 copy-start.1
  132.8 12.5 %here.3.remote = f32[256,128]{1,0:T(8,128)S(1)} custom-call(s32[192]{0:T(256)S(1)} %get-tuple-element.53.here_ids, s32[192]{0:T(256)S(1)} %get-tuple-element.52.there_ids, s32[1]{0:T(128)} %bitcast.35.count, f32[32,3,128,128]{3,2,1,0:T(8,128)} %get-tuple-element.42.cols_ref, bf16[64,112,128]{2,1,0:T(8,128)(2,1)S(1)} %get-tuple-element.45.wide_ref, ...), custom_call_target="tpu_custom_call" | custom-call | flops 10000000000 | bytes 1000000 | tf_op jit(solution)/shard_map/here/pallas_call | solution.py:335
  145.3 0.0 collective-permute-done.3.below
  145.3 0.0 all-to-all-done.3
  145.4 1.5 %last.1 = (f32[3,32,128]{2,1,0:T(8,128)}, f32[3,32,128]{2,1,0:T(8,128)}) custom-call(s32[64]{0:T(128)S(1)} %reshape_squeeze.3.exports, f32[256,128]{1,0:T(8,128)S(1)} %get-tuple-element.38.cells_ref, f32[256,128]{1,0:T(8,128)S(1)} %get-tuple-element.41.near, f32[256,128]{1,0:T(8,128)S(1)} %here.3.remote, f32[256,128]{1,0:T(8,128)S(1)} %collective-permute-done.3.below, ...), custom_call_target="tpu_custom_call" | custom-call | flops 100000000 | bytes 1000000 | tf_op jit(solution)/shard_map/last/pallas_call | solution.py:335
  (2 shorter events, 0.0 us)
Async XLA Ops:
  1.5 0.7 copy-start.2
  4.5 32.8 %all-to-all-start = ((f32[32,2,8,128]{3,2,1,0:T(8,128)}), f32[32,2,8,128]{3,2,1,0:T(8,128)S(1)}, u32[]{:S(2)}, u32[]{:S(2)}) async-start(f32[32,2,8,128]{3,2,1,0:T(8,128)} %bitcast.7), calls=%async_computation | async-start | bytes 524288 | tf_op jit(solution)/shard_map/all_to_all | solution.py:368
  17.4 5.4 %collective-permute-start = (f32[256,128]{1,0:T(8,128)S(1)}, f32[256,128]{1,0:T(8,128)S(1)}, u32[]{:S(2)}, u32[]{:S(2)}) collective-permute-start(f32[256,128]{1,0:T(8,128)S(1)} %get-tuple-element.27.cells_ref), channel_id=1, source_target_pairs={{0,32},{32,64},{64,96},{96,128},{128,160},{160,192},{192,224},{224... | collective-permute-start | bytes 393224 | tf_op jit(solution)/shard_map/ppermute | solution.py:30
  32.0 46.8 %collective-permute-start.1 = (f32[256,128]{1,0:T(8,128)S(1)}, f32[256,128]{1,0:T(8,128)S(1)}, u32[]{:S(2)}, u32[]{:S(2)}) collective-permute-start(f32[256,128]{1,0:T(8,128)S(1)} %get-tuple-element.36), channel_id=1, source_target_pairs={{32,0},{64,32},{96,64},{128,96},{160,128},{192,160},{224,192},{256... | collective-permute-start | bytes 393224 | tf_op jit(solution)/shard_map/ppermute | solution.py:30
  50.9 27.9 %all-to-all-start.1 = ((f32[32,2,8,128]{3,2,1,0:T(8,128)}), f32[32,2,8,128]{3,2,1,0:T(8,128)S(1)}, u32[]{:S(2)}, u32[]{:S(2)}) async-start(f32[32,2,8,128]{3,2,1,0:T(8,128)} %bitcast.13), calls=%async_computation.1 | async-start | bytes 524288 | tf_op jit(solution)/shard_map/all_to_all | solution.py:368
  80.4 10.9 %collective-permute-start.2 = (f32[256,128]{1,0:T(8,128)S(1)}, f32[256,128]{1,0:T(8,128)S(1)}, u32[]{:S(2)}, u32[]{:S(2)}) collective-permute-start(f32[256,128]{1,0:T(8,128)S(1)} %get-tuple-element.38.cells_ref), channel_id=1, source_target_pairs={{0,32},{32,64},{64,96},{96,128},{128,160},{160,192},{192,224},{224... | collective-permute-start | bytes 393224 | tf_op jit(solution)/shard_map/ppermute | solution.py:30
  82.3 21.3 %all-to-all-start.2 = ((f32[32,2,8,128]{3,2,1,0:T(8,128)}), f32[32,2,8,128]{3,2,1,0:T(8,128)S(1)}, u32[]{:S(2)}, u32[]{:S(2)}) async-start(f32[32,2,8,128]{3,2,1,0:T(8,128)} %bitcast.15), calls=%async_computation.2 | async-start | bytes 524288 | tf_op jit(solution)/shard_map/all_to_all | solution.py:368
  100.6 44.7 %collective-permute-start.3 = (f32[256,128]{1,0:T(8,128)S(1)}, f32[256,128]{1,0:T(8,128)S(1)}, u32[]{:S(2)}, u32[]{:S(2)}) collective-permute-start(f32[256,128]{1,0:T(8,128)S(1)} %get-tuple-element.47), channel_id=1, source_target_pairs={{32,0},{64,32},{96,64},{128,96},{160,128},{192,160},{224,192},{256... | collective-permute-start | bytes 393224 | tf_op jit(solution)/shard_map/ppermute | solution.py:30
  117.2 28.1 %all-to-all-start.3 = ((f32[32,2,8,128]{3,2,1,0:T(8,128)}), f32[32,2,8,128]{3,2,1,0:T(8,128)S(1)}, u32[]{:S(2)}, u32[]{:S(2)}) async-start(f32[32,2,8,128]{3,2,1,0:T(8,128)} %bitcast.17), calls=%async_computation.3 | async-start | bytes 524288 | tf_op jit(solution)/shard_map/all_to_all | solution.py:368
  132.8 12.5 %copy-start = (f32[1,32,3,128]{3,1,2,0:T(8,128)S(1)}, f32[1,32,3,128]{3,1,2,0:T(8,128)}, u32[]{:S(2)}) copy-start(f32[1,32,3,128]{3,1,2,0:T(8,128)} %param.7) | copy-start | bytes 147460
  132.8 12.5 %copy-start.1 = (f32[1,32,3,128]{3,1,2,0:T(8,128)S(1)}, f32[1,32,3,128]{3,1,2,0:T(8,128)}, u32[]{:S(2)}) copy-start(f32[1,32,3,128]{3,1,2,0:T(8,128)} %param.8) | copy-start | bytes 147460

commit v5 on v4

--- a/solution.py
+++ b/solution.py
@@ -18,8 +18,8 @@
 f32 = jnp.float32
 bf16 = jnp.bfloat16
 MOMENTS = 48
-UNROLL = 16
-HIDDEN = 8
+UNROLL = 32
+HIDDEN = 4
 NN = (((1,), (0,)), ((), ()))
 NT = (((1,), (1,)), ((), ()))
 
@@ -202,7 +202,7 @@
     half = wide_here.shape[0] // 2
     copies = []
     for part in range(2):
-        unrolled(half, 4, lambda c: cell(c + part * half))
+        unrolled(half, 8, lambda c: cell(c + part * half))
         rows = pl.ds(part * half, half)
         for k, (kept, out) in enumerate(((wide_here, wide_out), (cols_here, cols_out))):
             copies.append(pltpu.make_async_copy(kept.at[rows], out.at[rows], sems.at[part, k]))

time: 148 us -> 142 us (0.959)
  the two profiles are of different devices: /device:TPU:35 before, /device:TPU:31 now
where the time goes in v5:
time: 142 us; the launch traced here: 141 us
  Pallas kernels  70.6 us (50%)
  starting transfers between devices  66.2 us (47%)
  local copies, waits for them, and re-layouts  1.53 us (1%)
  between operations  1.5 us (1%)
    pallas_call x9, Pallas kernels, call(): pl.pallas_call(body, grid_spec=pltpu.PrefetchScalarGridSpec(num_scalar_pr...  70.6 us
    all_to_all x4, starting transfers between devices, exchange(): lax.all_to_all(value, 'cell', split_axis=0, concat_axis=0, tiled=True)  51.5 us
    ppermute x4, starting transfers between devices, shifted(): lax.ppermute(value, axis, [(source, source + steps) for source in range(l...  14.6 us
  transfers between devices with their start and end apart: 8, of which 1 were waited for; matrix products, arithmetic and copies ran while one was open for 0% of the time, Pallas kernels for 46%

profile of v5, /device:TPU:31, one launch (start us, length us, event | category | flops | bytes accessed | tf_op | source)
XLA Modules:
  0.0 141.1 jit_solution(10164633583755258372)
XLA Ops:
  0.6 0.8 copy.10
  1.4 0.1 reshape_squeeze.3.exports
  1.5 0.0 copy-start.2
  1.5 0.6 copy-done.2
  2.2 2.3 %pack.1 = (f32[256,128]{1,0:T(8,128)S(1)}, f32[512,128]{1,0:T(8,128)}) custom-call(s32[32]{0:T(128)S(1)} %bitcast.46, s32[64]{0:T(128)S(1)} %reshape_squeeze.3.exports, f32[1,3,32,128]{3,2,1,0:T(8,128)} %bitcast.42, f32[1,3,32,128]{3,2,1,0:T(8,128)} %bitcast.44), custom_call_target="tpu_custom_call" | custom-call | flops 100000000 | bytes 1000000 | tf_op jit(solution)/shard_map/pack/pallas_call | solution.py:335
  4.5 12.9 %all-to-all-start = ((f32[32,2,8,128]{3,2,1,0:T(8,128)}), f32[32,2,8,128]{3,2,1,0:T(8,128)S(1)}, u32[]{:S(2)}, u32[]{:S(2)}) async-start(f32[32,2,8,128]{3,2,1,0:T(8,128)} %bitcast.7), calls=%async_computation | async-start | bytes 524288 | tf_op jit(solution)/shard_map/all_to_all | solution.py:368
  17.4 5.5 %collective-permute-start = (f32[256,128]{1,0:T(8,128)S(1)}, f32[256,128]{1,0:T(8,128)S(1)}, u32[]{:S(2)}, u32[]{:S(2)}) collective-permute-start(f32[256,128]{1,0:T(8,128)S(1)} %get-tuple-element.27.cells_ref), channel_id=1, source_target_pairs={{0,32},{32,64},{64,96},{96,128},{128,160},{160,192},{192,224},{224... | collective-permute-start | bytes 393224 | tf_op jit(solution)/shard_map/ppermute | solution.py:30
  23.6 0.7 fusion
  24.3 0.6 collective-permute-done.above_ref
  24.8 7.6 %near.2 = (f32[256,128]{1,0:T(8,128)S(1)}, f32[256,128]{1,0:T(8,128)S(1)}, bf16[32,1,112,128]{3,2,1,0:T(8,128)(2,1)}, f32[32,3,128,128]{3,2,1,0:T(8,128)}) custom-call(f32[256,128]{1,0:T(8,128)S(1)} %get-tuple-element.27.cells_ref, f32[256,128]{1,0:T(8,128)S(1)} %collective-permute-done.above_ref), custom_call_target="tpu_custom_call" | custom-call | flops 10000000000 | bytes 1000000 | tf_op jit(solution)/shard_map/near/pallas_call | solution.py:335
  32.5 2.0 %collective-permute-start.1 = (f32[256,128]{1,0:T(8,128)S(1)}, f32[256,128]{1,0:T(8,128)S(1)}, u32[]{:S(2)}, u32[]{:S(2)}) collective-permute-start(f32[256,128]{1,0:T(8,128)S(1)} %get-tuple-element.36), channel_id=1, source_target_pairs={{32,0},{64,32},{96,64},{128,96},{160,128},{192,160},{224,192},{256... | collective-permute-start | bytes 393224 | tf_op jit(solution)/shard_map/ppermute | solution.py:30
  34.4 0.0 all-to-all-done
  34.5 13.1 %far.2 = (f32[512,128]{1,0:T(8,128)}, bf16[64,112,128]{2,1,0:T(8,128)(2,1)S(1)}, f32[1584,128]{1,0:T(8,128)}) custom-call(s32[192]{0:T(256)S(1)} %get-tuple-element.53.here_ids, s32[192]{0:T(256)S(1)} %get-tuple-element.52.there_ids, s32[1]{0:T(128)} %bitcast.32.count, bf16[32,1,112,128]{3,2,1,0:T(8,128)(2,1)} %get-tuple-element.32.wide_ref, ...), custom_call_target="tpu_custom_call" | custom-call | flops 10000000000 | bytes 1000000 | tf_op jit(solution)/shard_map/far/pallas_call | solution.py:335
  47.6 14.2 %all-to-all-start.1 = ((f32[32,2,8,128]{3,2,1,0:T(8,128)}), f32[32,2,8,128]{3,2,1,0:T(8,128)S(1)}, u32[]{:S(2)}, u32[]{:S(2)}) async-start(f32[32,2,8,128]{3,2,1,0:T(8,128)} %bitcast.13), calls=%async_computation.1 | async-start | bytes 524288 | tf_op jit(solution)/shard_map/all_to_all | solution.py:368
  61.7 11.9 %here.2.remote = f32[256,128]{1,0:T(8,128)S(1)} custom-call(s32[192]{0:T(256)S(1)} %get-tuple-element.53.here_ids, s32[192]{0:T(256)S(1)} %get-tuple-element.52.there_ids, s32[1]{0:T(128)} %bitcast.33.count, f32[32,3,128,128]{3,2,1,0:T(8,128)} %get-tuple-element.31.cols_ref, bf16[64,112,128]{2,1,0:T(8,128)(2,1)S(1)} %get-tuple-element.34.wide_ref, ...), custom_call_target="tpu_custom_call" | custom-call | flops 10000000000 | bytes 1000000 | tf_op jit(solution)/shard_map/here/pallas_call | solution.py:335
  73.6 0.0 collective-permute-done.1.below
  73.6 0.0 all-to-all-done.1
  73.6 1.6 %middle.1 = (f32[256,128]{1,0:T(8,128)S(1)}, f32[256,128]{1,0:T(8,128)S(1)}, f32[512,128]{1,0:T(8,128)}) custom-call(s32[64]{0:T(128)S(1)} %reshape_squeeze.3.exports, f32[256,128]{1,0:T(8,128)S(1)} %get-tuple-element.27.cells_ref, f32[256,128]{1,0:T(8,128)S(1)} %get-tuple-element.30.near, f32[256,128]{1,0:T(8,128)S(1)} %here.2.remote, ...), custom_call_target="tpu_custom_call" | custom-call | flops 100000000 | bytes 1000000 | tf_op jit(solution)/shard_map/middle/pallas_call | solution.py:335
  75.2 5.2 %collective-permute-start.2 = (f32[256,128]{1,0:T(8,128)S(1)}, f32[256,128]{1,0:T(8,128)S(1)}, u32[]{:S(2)}, u32[]{:S(2)}) collective-permute-start(f32[256,128]{1,0:T(8,128)S(1)} %get-tuple-element.38.cells_ref), channel_id=1, source_target_pairs={{0,32},{32,64},{64,96},{96,128},{128,160},{160,192},{192,224},{224... | collective-permute-start | bytes 393224 | tf_op jit(solution)/shard_map/ppermute | solution.py:30
  80.4 10.3 %all-to-all-start.2 = ((f32[32,2,8,128]{3,2,1,0:T(8,128)}), f32[32,2,8,128]{3,2,1,0:T(8,128)S(1)}, u32[]{:S(2)}, u32[]{:S(2)}) async-start(f32[32,2,8,128]{3,2,1,0:T(8,128)} %bitcast.15), calls=%async_computation.2 | async-start | bytes 524288 | tf_op jit(solution)/shard_map/all_to_all | solution.py:368
  90.8 0.0 collective-permute-done.2.above_ref
  90.8 7.6 %near.3 = (f32[256,128]{1,0:T(8,128)S(1)}, f32[256,128]{1,0:T(8,128)S(1)}, bf16[32,1,112,128]{3,2,1,0:T(8,128)(2,1)}, f32[32,3,128,128]{3,2,1,0:T(8,128)}) custom-call(f32[256,128]{1,0:T(8,128)S(1)} %get-tuple-element.38.cells_ref, f32[256,128]{1,0:T(8,128)S(1)} %collective-permute-done.2.above_ref), custom_call_target="tpu_custom_call" | custom-call | flops 10000000000 | bytes 1000000 | tf_op jit(solution)/shard_map/near/pallas_call | solution.py:335
  98.4 1.9 %collective-permute-start.3 = (f32[256,128]{1,0:T(8,128)S(1)}, f32[256,128]{1,0:T(8,128)S(1)}, u32[]{:S(2)}, u32[]{:S(2)}) collective-permute-start(f32[256,128]{1,0:T(8,128)S(1)} %get-tuple-element.47), channel_id=1, source_target_pairs={{32,0},{64,32},{96,64},{128,96},{160,128},{192,160},{224,192},{256... | collective-permute-start | bytes 393224 | tf_op jit(solution)/shard_map/ppermute | solution.py:30
  100.3 0.0 all-to-all-done.2
  100.4 13.1 %far.3 = (f32[512,128]{1,0:T(8,128)}, bf16[64,112,128]{2,1,0:T(8,128)(2,1)S(1)}, f32[1584,128]{1,0:T(8,128)}) custom-call(s32[192]{0:T(256)S(1)} %get-tuple-element.53.here_ids, s32[192]{0:T(256)S(1)} %get-tuple-element.52.there_ids, s32[1]{0:T(128)} %bitcast.34.count, bf16[32,1,112,128]{3,2,1,0:T(8,128)(2,1)} %get-tuple-element.43.wide_ref, ...), custom_call_target="tpu_custom_call" | custom-call | flops 10000000000 | bytes 1000000 | tf_op jit(solution)/shard_map/far/pallas_call | solution.py:335
  113.5 14.2 %all-to-all-start.3 = ((f32[32,2,8,128]{3,2,1,0:T(8,128)}), f32[32,2,8,128]{3,2,1,0:T(8,128)S(1)}, u32[]{:S(2)}, u32[]{:S(2)}) async-start(f32[32,2,8,128]{3,2,1,0:T(8,128)} %bitcast.17), calls=%async_computation.3 | async-start | bytes 524288 | tf_op jit(solution)/shard_map/all_to_all | solution.py:368
  127.6 0.0 copy-start
  127.6 0.0 copy-start.1
  127.7 11.9 %here.3.remote = f32[256,128]{1,0:T(8,128)S(1)} custom-call(s32[192]{0:T(256)S(1)} %get-tuple-element.53.here_ids, s32[192]{0:T(256)S(1)} %get-tuple-element.52.there_ids, s32[1]{0:T(128)} %bitcast.35.count, f32[32,3,128,128]{3,2,1,0:T(8,128)} %get-tuple-element.42.cols_ref, bf16[64,112,128]{2,1,0:T(8,128)(2,1)S(1)} %get-tuple-element.45.wide_ref, ...), custom_call_target="tpu_custom_call" | custom-call | flops 10000000000 | bytes 1000000 | tf_op jit(solution)/shard_map/here/pallas_call | solution.py:335
  139.5 0.0 collective-permute-done.3.below
  139.5 0.0 all-to-all-done.3
  139.6 1.5 %last.1 = (f32[3,32,128]{2,1,0:T(8,128)}, f32[3,32,128]{2,1,0:T(8,128)}) custom-call(s32[64]{0:T(128)S(1)} %reshape_squeeze.3.exports, f32[256,128]{1,0:T(8,128)S(1)} %get-tuple-element.38.cells_ref, f32[256,128]{1,0:T(8,128)S(1)} %get-tuple-element.41.near, f32[256,128]{1,0:T(8,128)S(1)} %here.3.remote, f32[256,128]{1,0:T(8,128)S(1)} %collective-permute-done.3.below, ...), custom_call_target="tpu_custom_call" | custom-call | flops 100000000 | bytes 1000000 | tf_op jit(solution)/shard_map/last/pallas_call | solution.py:335
  (2 shorter events, 0.0 us)
Async XLA Ops:
  1.5 0.7 copy-start.2
  4.5 30.0 %all-to-all-start = ((f32[32,2,8,128]{3,2,1,0:T(8,128)}), f32[32,2,8,128]{3,2,1,0:T(8,128)S(1)}, u32[]{:S(2)}, u32[]{:S(2)}) async-start(f32[32,2,8,128]{3,2,1,0:T(8,128)} %bitcast.7), calls=%async_computation | async-start | bytes 524288 | tf_op jit(solution)/shard_map/all_to_all | solution.py:368
  17.4 7.5 %collective-permute-start = (f32[256,128]{1,0:T(8,128)S(1)}, f32[256,128]{1,0:T(8,128)S(1)}, u32[]{:S(2)}, u32[]{:S(2)}) collective-permute-start(f32[256,128]{1,0:T(8,128)S(1)} %get-tuple-element.27.cells_ref), channel_id=1, source_target_pairs={{0,32},{32,64},{64,96},{96,128},{128,160},{160,192},{192,224},{224... | collective-permute-start | bytes 393224 | tf_op jit(solution)/shard_map/ppermute | solution.py:30
  32.5 41.1 %collective-permute-start.1 = (f32[256,128]{1,0:T(8,128)S(1)}, f32[256,128]{1,0:T(8,128)S(1)}, u32[]{:S(2)}, u32[]{:S(2)}) collective-permute-start(f32[256,128]{1,0:T(8,128)S(1)} %get-tuple-element.36), channel_id=1, source_target_pairs={{32,0},{64,32},{96,64},{128,96},{160,128},{192,160},{224,192},{256... | collective-permute-start | bytes 393224 | tf_op jit(solution)/shard_map/ppermute | solution.py:30
  47.6 26.1 %all-to-all-start.1 = ((f32[32,2,8,128]{3,2,1,0:T(8,128)}), f32[32,2,8,128]{3,2,1,0:T(8,128)S(1)}, u32[]{:S(2)}, u32[]{:S(2)}) async-start(f32[32,2,8,128]{3,2,1,0:T(8,128)} %bitcast.13), calls=%async_computation.1 | async-start | bytes 524288 | tf_op jit(solution)/shard_map/all_to_all | solution.py:368
  75.2 15.6 %collective-permute-start.2 = (f32[256,128]{1,0:T(8,128)S(1)}, f32[256,128]{1,0:T(8,128)S(1)}, u32[]{:S(2)}, u32[]{:S(2)}) collective-permute-start(f32[256,128]{1,0:T(8,128)S(1)} %get-tuple-element.38.cells_ref), channel_id=1, source_target_pairs={{0,32},{32,64},{64,96},{96,128},{128,160},{160,192},{192,224},{224... | collective-permute-start | bytes 393224 | tf_op jit(solution)/shard_map/ppermute | solution.py:30
  80.4 19.9 %all-to-all-start.2 = ((f32[32,2,8,128]{3,2,1,0:T(8,128)}), f32[32,2,8,128]{3,2,1,0:T(8,128)S(1)}, u32[]{:S(2)}, u32[]{:S(2)}) async-start(f32[32,2,8,128]{3,2,1,0:T(8,128)} %bitcast.15), calls=%async_computation.2 | async-start | bytes 524288 | tf_op jit(solution)/shard_map/all_to_all | solution.py:368
  98.4 41.1 %collective-permute-start.3 = (f32[256,128]{1,0:T(8,128)S(1)}, f32[256,128]{1,0:T(8,128)S(1)}, u32[]{:S(2)}, u32[]{:S(2)}) collective-permute-start(f32[256,128]{1,0:T(8,128)S(1)} %get-tuple-element.47), channel_id=1, source_target_pairs={{32,0},{64,32},{96,64},{128,96},{160,128},{192,160},{224,192},{256... | collective-permute-start | bytes 393224 | tf_op jit(solution)/shard_map/ppermute | solution.py:30
  113.5 26.1 %all-to-all-start.3 = ((f32[32,2,8,128]{3,2,1,0:T(8,128)}), f32[32,2,8,128]{3,2,1,0:T(8,128)S(1)}, u32[]{:S(2)}, u32[]{:S(2)}) async-start(f32[32,2,8,128]{3,2,1,0:T(8,128)} %bitcast.17), calls=%async_computation.3 | async-start | bytes 524288 | tf_op jit(solution)/shard_map/all_to_all | solution.py:368
  127.6 11.9 %copy-start = (f32[1,32,3,128]{3,1,2,0:T(8,128)S(1)}, f32[1,32,3,128]{3,1,2,0:T(8,128)}, u32[]{:S(2)}) copy-start(f32[1,32,3,128]{3,1,2,0:T(8,128)} %param.7) | copy-start | bytes 147460
  127.6 11.9 %copy-start.1 = (f32[1,32,3,128]{3,1,2,0:T(8,128)S(1)}, f32[1,32,3,128]{3,1,2,0:T(8,128)}, u32[]{:S(2)}) copy-start(f32[1,32,3,128]{3,1,2,0:T(8,128)} %param.8) | copy-start | bytes 147460
